TPU v7x, 256 devices: a whole 4x4x8 slice. The times are simulated.
256 devices in a mesh: ctx: 16 (over x, y_lo, core), exp: 16 (over z, y_hi).
Axes of the slice: x: 4, y: 4 (y_hi: 2, y_lo: 2; y = y_hi * 2 + y_lo), z: 8, core: 2. Of those that a mesh axis runs over, the one named last changes fastest.
Arguments:
- queries: bfloat16 [1024, 64, 512], P('ctx', 'exp'), may hold values from -17 to 17
- latent: bfloat16 [1024, 512], P('ctx'), may hold values from -2 to 2
- grad_out: bfloat16 [1024, 64, 512], P('ctx', 'exp'), may hold values from -6 to 6
- doc_ids: int32 [1024], P('ctx'), may hold values from 0 to 5, as said below
- tokens: bfloat16 [32768, 7168], P(('ctx', 'exp')), may hold values from -6 to 6
- token_grads: bfloat16 [32768, 7168], P(('ctx', 'exp')), may hold values from -1.5 to 1.5
- gate_values: float32 [32768, 8], P(('ctx', 'exp')), may hold values from 0.3 to 3
- expert_ids: int32 [32768, 8], P(('ctx', 'exp')), may hold values from 0 to 255, as said below
- gate_order: int32 [256, 128], P(('ctx', 'exp')), may hold values from 0 to 127, each once within a row
- w_gate: bfloat16 [16, 7168, 2048], P('exp', None, 'ctx'), may hold values from -0.0625 to 0.0625
- w_up: bfloat16 [16, 7168, 2048], P('exp', None, 'ctx'), may hold values from -0.0625 to 0.0625
- w_down: bfloat16 [16, 2048, 7168], P('exp', 'ctx'), may hold values from -0.125 to 0.125
Outputs:
- d_queries: bfloat16 [1024, 64, 512], P('ctx', 'exp')
- d_latent: bfloat16 [1024, 512], P('ctx')
- d_tokens: bfloat16 [32768, 7168], P(('ctx', 'exp'))
- d_gates: bfloat16 [32768, 8], P(('ctx', 'exp'))
Inputs may be any that keep to these rules, and one draw needn't show every extreme that they name: `doc_ids`: never falling along the sequence; every number below 6 occurs. `expert_ids`: each row names 8 different experts. For every index of ctx some expert below 16 is named by 2 or more rows of every device at that index. `gate_order`: each row holds every number below 128 once.
All inputs are finite; a program needn't handle non-finite values.
Results may differ from a plain program's by a relative error of at most 0.02.
Values may be sent and summed in bfloat16 or wider, within the bound.
A program may use at most 128 MiB of HBM per device.

v0:
```python
import jax
import jax.numpy as jnp
from jax import lax
from jax.sharding import PartitionSpec as P

SCALE_DIM = 192
CAP = 2


def passed_along(array, axis, by):
    count = lax.axis_size(axis)
    return lax.ppermute(array, axis, [(i, (i + by) % count) for i in range(count)])


def pass_keys(key_block):
    return passed_along(key_block, "ctx", 1)


def pass_grads(carried):
    return passed_along(carried.astype(jnp.bfloat16), "ctx", 1).astype(carried.dtype)


def attention_grads(queries, latent, grad_out, doc_ids):
    cycle_size = lax.axis_size("ctx")
    my_index = lax.axis_index("ctx")
    row_count = queries.shape[0]
    head_count = queries.shape[1]
    latent_width = queries.shape[2]
    softmax_scale = SCALE_DIM ** (-0.5)
    all_docs = lax.all_gather(doc_ids, "ctx", axis=0, tiled=True)

    def masked_scores(key_block, source):
        key_docs = lax.dynamic_slice_in_dim(all_docs, source * row_count, row_count)
        allowed = key_docs[None, :] == doc_ids[:, None]
        router_logits = softmax_scale * jnp.einsum(
            "qhl,kl->hqk", queries, key_block, preferred_element_type=jnp.float32
        )
        return jnp.where(allowed[None], router_logits, -1e30)

    def forward_visit(state, hop_index):
        key_block, prev_max, prev_sum, prev_out = state
        source = (my_index - hop_index) % cycle_size
        router_logits = masked_scores(key_block, source)
        new_max = jnp.maximum(prev_max, jnp.max(router_logits, axis=2))
        shrink = jnp.exp(prev_max - new_max)
        unnorm = jnp.exp(router_logits - new_max[:, :, None])
        new_sum = prev_sum * shrink + jnp.sum(unnorm, axis=2)
        new_out = prev_out * shrink[:, :, None] + jnp.einsum(
            "hqk,kl->hql",
            unnorm.astype(jnp.bfloat16),
            key_block,
            preferred_element_type=jnp.float32,
        )
        return (key_block, new_max, new_sum, new_out)

    def forward_hop(hop_index, state):
        state = forward_visit(state, hop_index)
        return (pass_keys(state[0]), state[1], state[2], state[3])

    start_state = (
        latent,
        jnp.full((head_count, row_count), -1e30, jnp.float32),
        jnp.zeros((head_count, row_count), jnp.float32),
        jnp.zeros((head_count, row_count, latent_width), jnp.float32),
    )
    state = lax.fori_loop(0, cycle_size - 1, forward_hop, start_state)
    state = forward_visit(state, cycle_size - 1)
    output = state[3] / state[2][:, :, None]
    log_sum = state[1] + jnp.log(state[2])
    delta_rows = jnp.einsum(
        "qhl,hql->hq", grad_out.astype(jnp.float32), output, precision=lax.Precision.HIGHEST
    )

    def backward_terms(key_block, source):
        router_logits = masked_scores(key_block, source)
        probs = jnp.exp(router_logits - log_sum[:, :, None])
        prob_grad = jnp.einsum(
            "qhl,kl->hqk", grad_out, key_block, preferred_element_type=jnp.float32
        )
        score_grad = (probs * (prob_grad - delta_rows[:, :, None])).astype(jnp.bfloat16)
        query_term = softmax_scale * jnp.einsum(
            "hqk,kl->qhl", score_grad, key_block, preferred_element_type=jnp.float32
        )
        latent_term = softmax_scale * jnp.einsum(
            "hqk,qhl->kl", score_grad, queries, preferred_element_type=jnp.float32
        )
        latent_term = latent_term + jnp.einsum(
            "hqk,qhl->kl", probs.astype(jnp.bfloat16), grad_out, preferred_element_type=jnp.float32
        )
        return (query_term, latent_term)

    query_start = jnp.zeros(queries.shape, jnp.float32)
    last_source = (my_index + 1) % cycle_size

    def carry_hop(hop_index, state):
        key_block, carried, query_acc = state
        source = (my_index - hop_index) % cycle_size
        query_term, latent_term = backward_terms(key_block, source)
        return (pass_keys(key_block), pass_grads(carried + latent_term), query_acc + query_term)

    state = lax.fori_loop(
        0, cycle_size - 1, carry_hop, (latent, jnp.zeros(latent.shape, jnp.float32), query_start)
    )
    query_term, latent_term = backward_terms(state[0], last_source)
    own_latent = pass_grads(state[1] + latent_term)
    query_acc = state[2] + query_term
    d_latent = lax.psum(own_latent.astype(jnp.bfloat16), "exp")
    return (query_acc.astype(jnp.bfloat16), d_latent)


def expert_grads(tokens, token_grads, gate_values, expert_ids, gate_order, w_gate, w_up, w_down):
    exp_size = lax.axis_size("exp")
    per_device = w_gate.shape[0]
    resident = per_device * exp_size
    model_width = tokens.shape[1]
    expert_span = jnp.arange(resident, dtype=jnp.int32)
    matches = (expert_ids[:, :, None] == expert_span).astype(jnp.int32)
    hits = jnp.sum(matches, axis=1)
    priority = gate_order[0]
    earlier = (priority[:, None] < priority[None, :]).astype(jnp.int32)
    ranks = jnp.einsum("ut,ue->te", earlier, hits)
    chosen = (hits[:, :, None] == 1) & (ranks[:, :, None] == jnp.arange(CAP, dtype=jnp.int32))
    picker = chosen.astype(jnp.bfloat16)
    send_in = jnp.einsum("tes,td->esd", picker, tokens, preferred_element_type=jnp.float32).astype(
        jnp.bfloat16
    )
    send_grad = jnp.einsum(
        "tes,td->esd", picker, token_grads, preferred_element_type=jnp.float32
    ).astype(jnp.bfloat16)
    recv_in, recv_grad = (
        lax.all_to_all(send_in, "exp", split_axis=0, concat_axis=0, tiled=True),
        lax.all_to_all(send_grad, "exp", split_axis=0, concat_axis=0, tiled=True),
    )
    recv_in = recv_in.reshape(exp_size, per_device, CAP, model_width)
    recv_grad = recv_grad.reshape(exp_size, per_device, CAP, model_width)
    piece_in = lax.all_gather(recv_in, "ctx", axis=0, tiled=True)
    piece_grad = lax.all_gather(recv_grad, "ctx", axis=0, tiled=True)
    gate_pre = jnp.einsum("necd,edh->nech", piece_in, w_gate, preferred_element_type=jnp.float32)
    up_pre = jnp.einsum("necd,edh->nech", piece_in, w_up, preferred_element_type=jnp.float32)
    act_grad = jnp.einsum("necd,ehd->nech", piece_grad, w_down, preferred_element_type=jnp.float32)
    gate_sig = jax.nn.sigmoid(gate_pre)
    silu_val = gate_pre * gate_sig
    hidden_act = (silu_val * up_pre).astype(jnp.bfloat16)
    score_part = jnp.sum(hidden_act.astype(jnp.float32) * act_grad, axis=3)
    gate_grad = (act_grad * up_pre * gate_sig * (1.0 + gate_pre * (1.0 - gate_sig))).astype(
        jnp.bfloat16
    )
    up_grad = (act_grad * silu_val).astype(jnp.bfloat16)
    term = jnp.einsum("nech,edh->necd", gate_grad, w_gate, preferred_element_type=jnp.float32)
    row_sums = lax.psum_scatter(
        (
            term + jnp.einsum("nech,edh->necd", up_grad, w_up, preferred_element_type=jnp.float32)
        ).astype(jnp.bfloat16),
        "ctx",
        scatter_dimension=0,
        tiled=True,
    )
    score_sums = lax.psum_scatter(score_part, "ctx", scatter_dimension=0, tiled=True)
    back_rows, back_scores = (
        lax.all_to_all(row_sums, "exp", split_axis=0, concat_axis=0, tiled=True),
        lax.all_to_all(
            score_sums.astype(jnp.bfloat16), "exp", split_axis=0, concat_axis=0, tiled=True
        ),
    )
    back_rows = back_rows.reshape(resident, CAP, model_width)
    back_scores = back_scores.reshape(resident, CAP)
    gate_mass = jnp.sum(matches.astype(jnp.float32) * gate_values[:, :, None], axis=1)
    weighting = chosen.astype(jnp.float32) * gate_mass[:, :, None]
    d_tokens = jnp.einsum(
        "tes,esd->td", weighting, back_rows.astype(jnp.float32), precision=lax.Precision.HIGHEST
    )
    kept_scores = jnp.einsum(
        "tes,es->te",
        chosen.astype(jnp.float32),
        back_scores.astype(jnp.float32),
        precision=lax.Precision.HIGHEST,
    )
    d_gates = jnp.einsum(
        "tke,te->tk", matches.astype(jnp.float32), kept_scores, precision=lax.Precision.HIGHEST
    )
    return (d_tokens.astype(jnp.bfloat16), d_gates.astype(jnp.bfloat16))


def local(
    queries,
    latent,
    grad_out,
    doc_ids,
    tokens,
    token_grads,
    gate_values,
    expert_ids,
    gate_order,
    w_gate,
    w_up,
    w_down,
):
    d_queries, d_latent = attention_grads(queries, latent, grad_out, doc_ids)
    d_tokens, d_gates = expert_grads(
        tokens, token_grads, gate_values, expert_ids, gate_order, w_gate, w_up, w_down
    )
    return (d_queries, d_latent, d_tokens, d_gates)


def solution(mesh):
    in_specs = (
        P("ctx", "exp", None),
        P("ctx", None),
        P("ctx", "exp", None),
        P("ctx"),
        P(("ctx", "exp"), None),
        P(("ctx", "exp"), None),
        P(("ctx", "exp"), None),
        P(("ctx", "exp"), None),
        P(("ctx", "exp"), None),
        P("exp", None, "ctx"),
        P("exp", None, "ctx"),
        P("exp", "ctx", None),
    )
    out_specs = (
        P("ctx", "exp", None),
        P("ctx", None),
        P(("ctx", "exp"), None),
        P(("ctx", "exp"), None),
    )
    return jax.shard_map(local, mesh=mesh, in_specs=in_specs, out_specs=out_specs, check_vma=False)
```

profile of v0, /device:TPU:2, one launch (start us, length us, event | category | flops | bytes accessed | tf_op | source)
XLA Modules:
  0.0 525.2 jit_solution(16147684486193947589)
XLA Ops:
  8.1 1.0 copy.161
  9.7 0.9 fusion.86
  10.7 1.9 convolution_convert_fusion
  13.1 28.4 %all_to_all.20 = bf16[16,2,7168]{2,1,0:T(2,128)(2,1)S(1)} all-to-all(bf16[16,2,7168]{2,1,0:T(2,128)(2,1)S(1)} %copy.73), channel_id=1, replica_groups=mesh['ctx'=16,'exp'=16] {'exp'}, dimensions={0} | all-to-all | bytes 917504 | tf_op jit(solution)/shard_map/all_to_all | solution.py:131
  41.4 0.8 copy.74
  42.3 1.9 convolution_convert_fusion.1
  44.3 1.3 copy.71
  45.5 4.2 all-to-all-start
  50.0 1.0 copy.65
  52.6 11.2 %all-reduce = s32[1024]{0:T(1024)} all-reduce(s32[1024]{0:T(1024)S(1)} %dynamic-update-slice), channel_id=1, replica_groups=mesh['ctx'=16,'exp'=16] {'ctx'}, use_global_device_ids=true, to_apply=%add | all-reduce | flops 1024 | bytes 8192
  63.8 0.8 fusion.106
  65.3 0.9 all-to-all-done
  66.1 1.9 copy.72
  68.3 82.0 %while.42 = (s32[]{:T(128)}, bf16[64,512]{1,0:T(8,128)(2,1)S(1)}, f32[4,64]{1,0:T(4,128)S(1)}, f32[4,64]{1,0:T(4,128)S(1)}, f32[4,64,512]{2,1,0:T(8,128)S(1)}, /...) while((s32[]{:T(128)}, bf16[64,512]{1,0:T(8,128)(2,1)S(1)}, ...), condition=%wide.region_3.4_spmd.clone, body=%wide.region_0.3_spmd.clone.sunk | while | flops 34067728 | bytes 2057580 | solution.py:66
  69.9 4.1 collective-permute-done
  75.5 4.1 collective-permute-done
  81.1 4.1 collective-permute-done
  86.8 3.9 collective-permute-done
  92.2 3.1 collective-permute-done
  96.8 3.1 collective-permute-done
  101.4 3.1 collective-permute-done
  106.0 3.1 collective-permute-done
  110.6 4.4 collective-permute-done
  116.5 4.4 collective-permute-done
  122.5 4.5 collective-permute-done
  128.5 4.5 collective-permute-done
  134.4 4.5 collective-permute-done
  140.4 4.4 collective-permute-done
  146.4 3.9 collective-permute-done
  150.3 1.3 fusion.107
  152.4 5.8 %fusion.49 = f32[256,1,2,128]{0,3,2,1:T(8,128)S(1)} fusion(bf16[256,2,7168]{2,0,1:T(8,128)(2,1)} %all-gather.7.cloned.1.call-done, bf16[1,7168,128]{2,1,0:T(8,128)(2,1)S(1)} %copy-done), kind=kOutput, calls=%fused_computation.64 | convolution fusion | flops 939524096 | bytes 9437184 | tf_op jit(solution)/shard_map/necd,edh->nech/dot_general | solution.py:138
  158.2 3.2 fusion.46
  161.4 6.3 %multiply_reduce_fusion.1 = (f32[256,2]{0,1:T(2,128)S(1)}, f32[256,1,2,128]{0,3,2,1:T(8,128)S(1)}) fusion(f32[256,1,2,128]{0,3,2,1:T(8,128)} %fusion.46, f32[256,1,2,128]{0,3,2,1:T(8,128)S(1)} %fusion.49, bf16[256,2,7168]{2,0,1:T(8,128)(2,1)} %all-gather.5.cloned.1.call-done, bf16[1,128,7168]{2,1,0:T(8,128)(2,1)} %param.27), kind=kOutput, calls=%fused_computation.86 | convolution fusion | flops 940113408 | bytes 9963520 | tf_op jit(solution)/shard_map/necd,ehd->nech/dot_general | solution.py:140
  167.7 7.3 %fusion.28 = f32[256,2,7168]{2,0,1:T(8,128)} fusion(bf16[1,7168,128]{2,1,0:T(8,128)(2,1)S(1)} %copy-done, f32[256,1,2,128]{0,3,2,1:T(8,128)S(1)} %fusion.49, f32[256,1,2,128]{0,3,2,1:T(8,128)S(1)} %get-tuple-element.694, f32[256,1,2,128]{0,3,2,1:T(8,128)S(1)} %copy-done.9), kind=kOutput, calls=%fused_computation.45 | convolution fusion | flops 940179456 | bytes 17301504 | tf_op jit(solution)/shard_map/nech,edh->necd/dot_general | solution.py:149
  176.2 10.8 %fusion.26 = bf16[256,1,2,7168]{3,0,2,1:T(8,128)(2,1)} fusion(f32[256,2,7168]{2,0,1:T(8,128)} %fusion.28, bf16[1,7168,128]{2,1,0:T(8,128)(2,1)} %param.26, f32[256,1,2,128]{0,3,2,1:T(8,128)S(1)} %get-tuple-element.694, f32[256,1,2,128]{0,3,2,1:T(8,128)S(1)} %fusion.49), kind=kOutput, calls=%fused_computation.40 | convolution fusion | flops 947257344 | bytes 24379392 | tf_op jit(solution)/shard_map/nech,edh->necd/dot_general | solution.py:152
  187.9 113.3 %while.43 = (s32[]{:T(128)}, bf16[64,512]{1,0:T(8,128)(2,1)S(1)}, f32[64,512]{1,0:T(8,128)S(1)}, f32[64,4,512]{2,0,1:T(8,128)S(1)}, s32[]{:T(128)}, /*index=5*/s...) while((s32[]{:T(128)}, bf16[64,512]{1,0:T(8,128)(2,1)S(1)}, ...), condition=%wide.region_7.8_spmd.clone, body=%wide.region_6.7_spmd.clone.sunk | while | flops 84594704 | bytes 3911075 | solution.py:101
  190.2 4.3 collective-permute-done.2
  196.8 4.3 collective-permute-done.2
  203.5 4.3 collective-permute-done.2
  210.1 4.3 collective-permute-done.2
  216.8 4.3 collective-permute-done.2
  223.4 4.3 collective-permute-done.2
  230.1 4.3 collective-permute-done.2
  236.7 5.0 collective-permute-done.2
  244.0 5.5 %collective-permute-done.2 = bf16[64,512]{1,0:T(8,128)(2,1)S(1)} collective-permute-done((bf16[64,512]{1,0:T(8,128)(2,1)S(1)}, bf16[64,512]{1,0:T(8,128)(2,1)S(1)}, u32[]{:S(2)}, u32[]{:S(2)}) %collective-permute-start.2) | collective-permute-done | bytes 65568 | tf_op jit(solution)/shard_map/while/body/eval_jaxpr/ppermute | solution.py:12
  251.9 5.5 %collective-permute-done.2 = bf16[64,512]{1,0:T(8,128)(2,1)S(1)} collective-permute-done((bf16[64,512]{1,0:T(8,128)(2,1)S(1)}, bf16[64,512]{1,0:T(8,128)(2,1)S(1)}, u32[]{:S(2)}, u32[]{:S(2)}) %collective-permute-start.2) | collective-permute-done | bytes 65568 | tf_op jit(solution)/shard_map/while/body/eval_jaxpr/ppermute | solution.py:12
  259.7 6.3 %collective-permute-done.2 = bf16[64,512]{1,0:T(8,128)(2,1)S(1)} collective-permute-done((bf16[64,512]{1,0:T(8,128)(2,1)S(1)}, bf16[64,512]{1,0:T(8,128)(2,1)S(1)}, u32[]{:S(2)}, u32[]{:S(2)}) %collective-permute-start.2) | collective-permute-done | bytes 65568 | tf_op jit(solution)/shard_map/while/body/eval_jaxpr/ppermute | solution.py:12
  268.0 1.8 collective-permute-start.2
  270.1 7.2 %collective-permute-done.2 = bf16[64,512]{1,0:T(8,128)(2,1)S(1)} collective-permute-done((bf16[64,512]{1,0:T(8,128)(2,1)S(1)}, bf16[64,512]{1,0:T(8,128)(2,1)S(1)}, u32[]{:S(2)}, u32[]{:S(2)}) %collective-permute-start.2) | collective-permute-done | bytes 65568 | tf_op jit(solution)/shard_map/while/body/eval_jaxpr/ppermute | solution.py:12
  279.6 5.0 collective-permute-done.2
  286.6 1.8 collective-permute-start.2
  288.7 3.6 collective-permute-done.2
  294.3 2.6 collective-permute-start.2
  297.2 3.9 collective-permute-done.2
  301.2 1.2 fusion.60
  304.4 14.4 %all-to-all-start.3 = ((bf16[16,1,2]{2,1,0:T(2,128)(2,1)}), bf16[16,1,2]{2,1,0:T(2,128)(2,1)S(1)}, u32[]{:S(2)}, u32[]{:S(2)}) async-start(bf16[16,1,2]{2,1,0:T(2,128)(2,1)} %copy.81), calls=%async_computation.4 | async-start | bytes 16384 | tf_op jit(solution)/shard_map/all_to_all | solution.py:161
  318.8 20.8 %reduce-scatter.5.cloned.1.call-done = bf16[16,1,2,7168]{3,0,2,1:T(8,128)(2,1)} async-done(((bf16[256,1,2,7168]{3,0,2,1:T(8,128)(2,1)}), bf16[16,1,2,7168]{3,0,2,1:T(8,128)(2,1)}) %reduce-scatter.5.cloned.1.call-update) | async-done | bytes 458768 | tf_op jit(solution)/shard_map/reduce_scatter | solution.py:150
  339.6 2.3 copy.79
  341.9 10.6 %all-to-all-start.2 = ((bf16[16,1,2,7168]{3,2,1,0:T(2,128)(2,1)}), bf16[16,1,2,7168]{3,2,1,0:T(2,128)(2,1)S(1)}, u32[]{:S(2)}, u32[]{:S(2)}) async-start(bf16[16,1,2,7168]{3,2,1,0:T(2,128)(2,1)} %copy.79), calls=%async_computation.3 | async-start | bytes 917504 | tf_op jit(solution)/shard_map/all_to_all | solution.py:160
  352.8 1.4 collective-permute-start.3
  354.5 0.9 copy.83
  355.4 2.3 collective-permute-done.3
  359.1 153.7 %all-reduce.3.cloned.1.call-done = bf16[64,512]{1,0:T(8,128)(2,1)} async-done(((bf16[64,512]{1,0:T(8,128)(2,1)}), bf16[64,512]{1,0:T(8,128)(2,1)}) %all-reduce.3.cloned.1.call-update) | async-done | bytes 65552 | tf_op jit(solution)/shard_map/psum | solution.py:107
  514.5 2.9 fusion.27
  (413 shorter events, 67.4 us)
Async XLA Ops:
  8.0 144.4 %copy-start = (bf16[1,7168,128]{2,1,0:T(8,128)(2,1)S(1)}, bf16[1,7168,128]{2,1,0:T(8,128)(2,1)}, u32[]{:S(2)}) copy-start(bf16[1,7168,128]{2,1,0:T(8,128)(2,1)} %param.25) | copy-start | bytes 5505028
  8.0 144.4 %all-gather.7.cloned.1.call-start = ((), (), s32[]{:S(2)}) async-start(), calls=%async_computation.9 | async-start | bytes 7798784 | tf_op jit(solution)/shard_map/all_gather | solution.py:136
  9.0 41.0 %copy-start.3 = (bf16[64,512]{1,0:T(8,128)(2,1)}, bf16[64,512]{1,0:T(8,128)(2,1)S(1)}, u32[]{:S(2)}) copy-start(bf16[64,512]{1,0:T(8,128)(2,1)S(1)} %copy.161) | copy-start | bytes 196612
  42.3 7.6 %copy-start.10 = (bf16[64,4,512]{2,1,0:T(4,128)(2,1)S(1)}, bf16[64,4,512]{2,1,0:T(4,128)(2,1)}, u32[]{:S(2)}) copy-start(bf16[64,4,512]{2,1,0:T(4,128)(2,1)} %param.16) | copy-start | bytes 786436
  44.2 6.8 %copy-start.18 = (u32[256]{0:T(256)S(1)}, u32[256]{0:T(256)}, u32[]{:S(2)}) copy-start(u32[256]{0:T(256)} %constant.237) | copy-start | bytes 3076
  44.2 8.1 %copy-start.14 = (s32[64]{0:T(128)S(1)}, s32[64]{0:T(128)}, u32[]{:S(2)}) copy-start(s32[64]{0:T(128)} %param.19) | copy-start | bytes 772
  45.5 20.6 %all-to-all-start = ((bf16[16,2,7168]{2,1,0:T(2,128)(2,1)}), bf16[16,2,7168]{2,1,0:T(2,128)(2,1)}, u32[]{:S(2)}, u32[]{:S(2)}) async-start(bf16[16,2,7168]{2,1,0:T(2,128)(2,1)} %copy.71), calls=%async_computation | async-start | bytes 917504 | tf_op jit(solution)/shard_map/all_to_all | solution.py:132
  49.8 111.7 %all-gather.5.cloned.1.call-start = ((), (), s32[]{:S(2)}) async-start(), calls=%async_computation.8 | async-start | bytes 7798784 | tf_op jit(solution)/shard_map/all_gather | solution.py:137
  50.0 18.2 %copy-start.5 = (bf16[64,512]{1,0:T(8,128)(2,1)S(1)}, bf16[64,512]{1,0:T(8,128)(2,1)}, u32[]{:S(2)}) copy-start(bf16[64,512]{1,0:T(8,128)(2,1)} %copy-done.3) | copy-start | bytes 196612
  68.0 234.9 %reduce-scatter.7.cloned.1.call-start = ((), (), s32[]{:S(2)}) async-start(), calls=%async_computation.10 | async-start | bytes 139264
  68.3 5.7 %collective-permute-start = (bf16[64,512]{1,0:T(8,128)(2,1)S(1)}, bf16[64,512]{1,0:T(8,128)(2,1)S(1)}, u32[]{:S(2)}, u32[]{:S(2)}) collective-permute-start(bf16[64,512]{1,0:T(8,128)(2,1)S(1)} %copy.137), channel_id=1, source_target_pairs={{0,16},{16,32},{32,48},{48,64},{64,80},{80,96},{96,112},{112,128},... | collective-permute-start | bytes 196616 | tf_op jit(solution)/shard_map/while/body/eval_jaxpr/ppermute | solution.py:12
  74.0 5.6 %collective-permute-start = (bf16[64,512]{1,0:T(8,128)(2,1)S(1)}, bf16[64,512]{1,0:T(8,128)(2,1)S(1)}, u32[]{:S(2)}, u32[]{:S(2)}) collective-permute-start(bf16[64,512]{1,0:T(8,128)(2,1)S(1)} %copy.137), channel_id=1, source_target_pairs={{0,16},{16,32},{32,48},{48,64},{64,80},{80,96},{96,112},{112,128},... | collective-permute-start | bytes 196616 | tf_op jit(solution)/shard_map/while/body/eval_jaxpr/ppermute | solution.py:12
  79.6 5.6 %collective-permute-start = (bf16[64,512]{1,0:T(8,128)(2,1)S(1)}, bf16[64,512]{1,0:T(8,128)(2,1)S(1)}, u32[]{:S(2)}, u32[]{:S(2)}) collective-permute-start(bf16[64,512]{1,0:T(8,128)(2,1)S(1)} %copy.137), channel_id=1, source_target_pairs={{0,16},{16,32},{32,48},{48,64},{64,80},{80,96},{96,112},{112,128},... | collective-permute-start | bytes 196616 | tf_op jit(solution)/shard_map/while/body/eval_jaxpr/ppermute | solution.py:12
  85.2 5.4 %collective-permute-start = (bf16[64,512]{1,0:T(8,128)(2,1)S(1)}, bf16[64,512]{1,0:T(8,128)(2,1)S(1)}, u32[]{:S(2)}, u32[]{:S(2)}) collective-permute-start(bf16[64,512]{1,0:T(8,128)(2,1)S(1)} %copy.137), channel_id=1, source_target_pairs={{0,16},{16,32},{32,48},{48,64},{64,80},{80,96},{96,112},{112,128},... | collective-permute-start | bytes 196616 | tf_op jit(solution)/shard_map/while/body/eval_jaxpr/ppermute | solution.py:12
  90.7 4.6 collective-permute-start
  95.3 4.6 collective-permute-start
  99.9 4.6 collective-permute-start
  104.5 4.6 collective-permute-start
  109.1 5.9 %collective-permute-start = (bf16[64,512]{1,0:T(8,128)(2,1)S(1)}, bf16[64,512]{1,0:T(8,128)(2,1)S(1)}, u32[]{:S(2)}, u32[]{:S(2)}) collective-permute-start(bf16[64,512]{1,0:T(8,128)(2,1)S(1)} %copy.137), channel_id=1, source_target_pairs={{0,16},{16,32},{32,48},{48,64},{64,80},{80,96},{96,112},{112,128},... | collective-permute-start | bytes 196616 | tf_op jit(solution)/shard_map/while/body/eval_jaxpr/ppermute | solution.py:12
  115.0 6.0 %collective-permute-start = (bf16[64,512]{1,0:T(8,128)(2,1)S(1)}, bf16[64,512]{1,0:T(8,128)(2,1)S(1)}, u32[]{:S(2)}, u32[]{:S(2)}) collective-permute-start(bf16[64,512]{1,0:T(8,128)(2,1)S(1)} %copy.137), channel_id=1, source_target_pairs={{0,16},{16,32},{32,48},{48,64},{64,80},{80,96},{96,112},{112,128},... | collective-permute-start | bytes 196616 | tf_op jit(solution)/shard_map/while/body/eval_jaxpr/ppermute | solution.py:12
  121.0 6.0 %collective-permute-start = (bf16[64,512]{1,0:T(8,128)(2,1)S(1)}, bf16[64,512]{1,0:T(8,128)(2,1)S(1)}, u32[]{:S(2)}, u32[]{:S(2)}) collective-permute-start(bf16[64,512]{1,0:T(8,128)(2,1)S(1)} %copy.137), channel_id=1, source_target_pairs={{0,16},{16,32},{32,48},{48,64},{64,80},{80,96},{96,112},{112,128},... | collective-permute-start | bytes 196616 | tf_op jit(solution)/shard_map/while/body/eval_jaxpr/ppermute | solution.py:12
  127.0 6.0 %collective-permute-start = (bf16[64,512]{1,0:T(8,128)(2,1)S(1)}, bf16[64,512]{1,0:T(8,128)(2,1)S(1)}, u32[]{:S(2)}, u32[]{:S(2)}) collective-permute-start(bf16[64,512]{1,0:T(8,128)(2,1)S(1)} %copy.137), channel_id=1, source_target_pairs={{0,16},{16,32},{32,48},{48,64},{64,80},{80,96},{96,112},{112,128},... | collective-permute-start | bytes 196616 | tf_op jit(solution)/shard_map/while/body/eval_jaxpr/ppermute | solution.py:12
  132.9 6.0 %collective-permute-start = (bf16[64,512]{1,0:T(8,128)(2,1)S(1)}, bf16[64,512]{1,0:T(8,128)(2,1)S(1)}, u32[]{:S(2)}, u32[]{:S(2)}) collective-permute-start(bf16[64,512]{1,0:T(8,128)(2,1)S(1)} %copy.137), channel_id=1, source_target_pairs={{0,16},{16,32},{32,48},{48,64},{64,80},{80,96},{96,112},{112,128},... | collective-permute-start | bytes 196616 | tf_op jit(solution)/shard_map/while/body/eval_jaxpr/ppermute | solution.py:12
  138.9 6.0 %collective-permute-start = (bf16[64,512]{1,0:T(8,128)(2,1)S(1)}, bf16[64,512]{1,0:T(8,128)(2,1)S(1)}, u32[]{:S(2)}, u32[]{:S(2)}) collective-permute-start(bf16[64,512]{1,0:T(8,128)(2,1)S(1)} %copy.137), channel_id=1, source_target_pairs={{0,16},{16,32},{32,48},{48,64},{64,80},{80,96},{96,112},{112,128},... | collective-permute-start | bytes 196616 | tf_op jit(solution)/shard_map/while/body/eval_jaxpr/ppermute | solution.py:12
  144.9 5.4 %collective-permute-start = (bf16[64,512]{1,0:T(8,128)(2,1)S(1)}, bf16[64,512]{1,0:T(8,128)(2,1)S(1)}, u32[]{:S(2)}, u32[]{:S(2)}) collective-permute-start(bf16[64,512]{1,0:T(8,128)(2,1)S(1)} %copy.137), channel_id=1, source_target_pairs={{0,16},{16,32},{32,48},{48,64},{64,80},{80,96},{96,112},{112,128},... | collective-permute-start | bytes 196616 | tf_op jit(solution)/shard_map/while/body/eval_jaxpr/ppermute | solution.py:12
  175.9 163.8 %reduce-scatter.5.cloned.1.call-start = ((), (), s32[]{:S(2)}) async-start(), calls=%async_computation.7 | async-start | bytes 7798784 | tf_op jit(solution)/shard_map/reduce_scatter | solution.py:150
  187.9 114.5 %copy-start.8 = (bf16[64,4,512]{2,1,0:T(4,128)(2,1)S(1)}, bf16[64,4,512]{2,1,0:T(4,128)(2,1)}, u32[]{:S(2)}) copy-start(bf16[64,4,512]{2,1,0:T(4,128)(2,1)} %param.18) | copy-start | bytes 786436
  187.9 6.6 %collective-permute-start.1 = (bf16[64,512]{1,0:T(8,128)(2,1)S(1)}, bf16[64,512]{1,0:T(8,128)(2,1)S(1)}, u32[]{:S(2)}, u32[]{:S(2)}) collective-permute-start(bf16[64,512]{1,0:T(8,128)(2,1)S(1)} %copy.151), channel_id=1, source_target_pairs={{0,16},{16,32},{32,48},{48,64},{64,80},{80,96},{96,112},{112,128},... | collective-permute-start | bytes 196616 | tf_op jit(solution)/shard_map/while/body/eval_jaxpr/ppermute | solution.py:12
  189.8 4.7 collective-permute-start.2
  194.5 6.6 %collective-permute-start.1 = (bf16[64,512]{1,0:T(8,128)(2,1)S(1)}, bf16[64,512]{1,0:T(8,128)(2,1)S(1)}, u32[]{:S(2)}, u32[]{:S(2)}) collective-permute-start(bf16[64,512]{1,0:T(8,128)(2,1)S(1)} %copy.151), channel_id=1, source_target_pairs={{0,16},{16,32},{32,48},{48,64},{64,80},{80,96},{96,112},{112,128},... | collective-permute-start | bytes 196616 | tf_op jit(solution)/shard_map/while/body/eval_jaxpr/ppermute | solution.py:12
  196.4 4.7 collective-permute-start.2
  201.2 6.6 %collective-permute-start.1 = (bf16[64,512]{1,0:T(8,128)(2,1)S(1)}, bf16[64,512]{1,0:T(8,128)(2,1)S(1)}, u32[]{:S(2)}, u32[]{:S(2)}) collective-permute-start(bf16[64,512]{1,0:T(8,128)(2,1)S(1)} %copy.151), channel_id=1, source_target_pairs={{0,16},{16,32},{32,48},{48,64},{64,80},{80,96},{96,112},{112,128},... | collective-permute-start | bytes 196616 | tf_op jit(solution)/shard_map/while/body/eval_jaxpr/ppermute | solution.py:12
  203.1 4.7 collective-permute-start.2
  207.8 6.6 %collective-permute-start.1 = (bf16[64,512]{1,0:T(8,128)(2,1)S(1)}, bf16[64,512]{1,0:T(8,128)(2,1)S(1)}, u32[]{:S(2)}, u32[]{:S(2)}) collective-permute-start(bf16[64,512]{1,0:T(8,128)(2,1)S(1)} %copy.151), channel_id=1, source_target_pairs={{0,16},{16,32},{32,48},{48,64},{64,80},{80,96},{96,112},{112,128},... | collective-permute-start | bytes 196616 | tf_op jit(solution)/shard_map/while/body/eval_jaxpr/ppermute | solution.py:12
  209.7 4.7 collective-permute-start.2
  214.5 6.6 %collective-permute-start.1 = (bf16[64,512]{1,0:T(8,128)(2,1)S(1)}, bf16[64,512]{1,0:T(8,128)(2,1)S(1)}, u32[]{:S(2)}, u32[]{:S(2)}) collective-permute-start(bf16[64,512]{1,0:T(8,128)(2,1)S(1)} %copy.151), channel_id=1, source_target_pairs={{0,16},{16,32},{32,48},{48,64},{64,80},{80,96},{96,112},{112,128},... | collective-permute-start | bytes 196616 | tf_op jit(solution)/shard_map/while/body/eval_jaxpr/ppermute | solution.py:12
  216.4 4.7 collective-permute-start.2
  221.1 6.6 %collective-permute-start.1 = (bf16[64,512]{1,0:T(8,128)(2,1)S(1)}, bf16[64,512]{1,0:T(8,128)(2,1)S(1)}, u32[]{:S(2)}, u32[]{:S(2)}) collective-permute-start(bf16[64,512]{1,0:T(8,128)(2,1)S(1)} %copy.151), channel_id=1, source_target_pairs={{0,16},{16,32},{32,48},{48,64},{64,80},{80,96},{96,112},{112,128},... | collective-permute-start | bytes 196616 | tf_op jit(solution)/shard_map/while/body/eval_jaxpr/ppermute | solution.py:12
  223.0 4.7 collective-permute-start.2
  227.8 6.6 %collective-permute-start.1 = (bf16[64,512]{1,0:T(8,128)(2,1)S(1)}, bf16[64,512]{1,0:T(8,128)(2,1)S(1)}, u32[]{:S(2)}, u32[]{:S(2)}) collective-permute-start(bf16[64,512]{1,0:T(8,128)(2,1)S(1)} %copy.151), channel_id=1, source_target_pairs={{0,16},{16,32},{32,48},{48,64},{64,80},{80,96},{96,112},{112,128},... | collective-permute-start | bytes 196616 | tf_op jit(solution)/shard_map/while/body/eval_jaxpr/ppermute | solution.py:12
  229.7 4.7 collective-permute-start.2
  234.4 7.3 %collective-permute-start.1 = (bf16[64,512]{1,0:T(8,128)(2,1)S(1)}, bf16[64,512]{1,0:T(8,128)(2,1)S(1)}, u32[]{:S(2)}, u32[]{:S(2)}) collective-permute-start(bf16[64,512]{1,0:T(8,128)(2,1)S(1)} %copy.151), channel_id=1, source_target_pairs={{0,16},{16,32},{32,48},{48,64},{64,80},{80,96},{96,112},{112,128},... | collective-permute-start | bytes 196616 | tf_op jit(solution)/shard_map/while/body/eval_jaxpr/ppermute | solution.py:12
  236.3 5.4 %collective-permute-start.2 = (bf16[64,512]{1,0:T(8,128)(2,1)S(1)}, bf16[64,512]{1,0:T(8,128)(2,1)S(1)}, u32[]{:S(2)}, u32[]{:S(2)}) collective-permute-start(bf16[64,512]{1,0:T(8,128)(2,1)S(1)} %fusion.162), channel_id=1, source_target_pairs={{0,16},{16,32},{32,48},{48,64},{64,80},{80,96},{96,112},{112,128},... | collective-permute-start | bytes 196616 | tf_op jit(solution)/shard_map/while/body/eval_jaxpr/ppermute | solution.py:12
  241.7 7.8 %collective-permute-start.1 = (bf16[64,512]{1,0:T(8,128)(2,1)S(1)}, bf16[64,512]{1,0:T(8,128)(2,1)S(1)}, u32[]{:S(2)}, u32[]{:S(2)}) collective-permute-start(bf16[64,512]{1,0:T(8,128)(2,1)S(1)} %copy.151), channel_id=1, source_target_pairs={{0,16},{16,32},{32,48},{48,64},{64,80},{80,96},{96,112},{112,128},... | collective-permute-start | bytes 196616 | tf_op jit(solution)/shard_map/while/body/eval_jaxpr/ppermute | solution.py:12
  243.6 5.9 %collective-permute-start.2 = (bf16[64,512]{1,0:T(8,128)(2,1)S(1)}, bf16[64,512]{1,0:T(8,128)(2,1)S(1)}, u32[]{:S(2)}, u32[]{:S(2)}) collective-permute-start(bf16[64,512]{1,0:T(8,128)(2,1)S(1)} %fusion.162), channel_id=1, source_target_pairs={{0,16},{16,32},{32,48},{48,64},{64,80},{80,96},{96,112},{112,128},... | collective-permute-start | bytes 196616 | tf_op jit(solution)/shard_map/while/body/eval_jaxpr/ppermute | solution.py:12
  249.6 7.8 %collective-permute-start.1 = (bf16[64,512]{1,0:T(8,128)(2,1)S(1)}, bf16[64,512]{1,0:T(8,128)(2,1)S(1)}, u32[]{:S(2)}, u32[]{:S(2)}) collective-permute-start(bf16[64,512]{1,0:T(8,128)(2,1)S(1)} %copy.151), channel_id=1, source_target_pairs={{0,16},{16,32},{32,48},{48,64},{64,80},{80,96},{96,112},{112,128},... | collective-permute-start | bytes 196616 | tf_op jit(solution)/shard_map/while/body/eval_jaxpr/ppermute | solution.py:12
  251.5 5.9 %collective-permute-start.2 = (bf16[64,512]{1,0:T(8,128)(2,1)S(1)}, bf16[64,512]{1,0:T(8,128)(2,1)S(1)}, u32[]{:S(2)}, u32[]{:S(2)}) collective-permute-start(bf16[64,512]{1,0:T(8,128)(2,1)S(1)} %fusion.162), channel_id=1, source_target_pairs={{0,16},{16,32},{32,48},{48,64},{64,80},{80,96},{96,112},{112,128},... | collective-permute-start | bytes 196616 | tf_op jit(solution)/shard_map/while/body/eval_jaxpr/ppermute | solution.py:12
  257.4 8.6 %collective-permute-start.1 = (bf16[64,512]{1,0:T(8,128)(2,1)S(1)}, bf16[64,512]{1,0:T(8,128)(2,1)S(1)}, u32[]{:S(2)}, u32[]{:S(2)}) collective-permute-start(bf16[64,512]{1,0:T(8,128)(2,1)S(1)} %copy.151), channel_id=1, source_target_pairs={{0,16},{16,32},{32,48},{48,64},{64,80},{80,96},{96,112},{112,128},... | collective-permute-start | bytes 196616 | tf_op jit(solution)/shard_map/while/body/eval_jaxpr/ppermute | solution.py:12
  259.3 6.7 %collective-permute-start.2 = (bf16[64,512]{1,0:T(8,128)(2,1)S(1)}, bf16[64,512]{1,0:T(8,128)(2,1)S(1)}, u32[]{:S(2)}, u32[]{:S(2)}) collective-permute-start(bf16[64,512]{1,0:T(8,128)(2,1)S(1)} %fusion.162), channel_id=1, source_target_pairs={{0,16},{16,32},{32,48},{48,64},{64,80},{80,96},{96,112},{112,128},... | collective-permute-start | bytes 196616 | tf_op jit(solution)/shard_map/while/body/eval_jaxpr/ppermute | solution.py:12
  266.1 11.2 %collective-permute-start.1 = (bf16[64,512]{1,0:T(8,128)(2,1)S(1)}, bf16[64,512]{1,0:T(8,128)(2,1)S(1)}, u32[]{:S(2)}, u32[]{:S(2)}) collective-permute-start(bf16[64,512]{1,0:T(8,128)(2,1)S(1)} %copy.151), channel_id=1, source_target_pairs={{0,16},{16,32},{32,48},{48,64},{64,80},{80,96},{96,112},{112,128},... | collective-permute-start | bytes 196616 | tf_op jit(solution)/shard_map/while/body/eval_jaxpr/ppermute | solution.py:12
  268.0 9.2 %collective-permute-start.2 = (bf16[64,512]{1,0:T(8,128)(2,1)S(1)}, bf16[64,512]{1,0:T(8,128)(2,1)S(1)}, u32[]{:S(2)}, u32[]{:S(2)}) collective-permute-start(bf16[64,512]{1,0:T(8,128)(2,1)S(1)} %fusion.162), channel_id=1, source_target_pairs={{0,16},{16,32},{32,48},{48,64},{64,80},{80,96},{96,112},{112,128},... | collective-permute-start | bytes 196616 | tf_op jit(solution)/shard_map/while/body/eval_jaxpr/ppermute | solution.py:12
  277.3 7.3 %collective-permute-start.1 = (bf16[64,512]{1,0:T(8,128)(2,1)S(1)}, bf16[64,512]{1,0:T(8,128)(2,1)S(1)}, u32[]{:S(2)}, u32[]{:S(2)}) collective-permute-start(bf16[64,512]{1,0:T(8,128)(2,1)S(1)} %copy.151), channel_id=1, source_target_pairs={{0,16},{16,32},{32,48},{48,64},{64,80},{80,96},{96,112},{112,128},... | collective-permute-start | bytes 196616 | tf_op jit(solution)/shard_map/while/body/eval_jaxpr/ppermute | solution.py:12
  279.2 5.4 %collective-permute-start.2 = (bf16[64,512]{1,0:T(8,128)(2,1)S(1)}, bf16[64,512]{1,0:T(8,128)(2,1)S(1)}, u32[]{:S(2)}, u32[]{:S(2)}) collective-permute-start(bf16[64,512]{1,0:T(8,128)(2,1)S(1)} %fusion.162), channel_id=1, source_target_pairs={{0,16},{16,32},{32,48},{48,64},{64,80},{80,96},{96,112},{112,128},... | collective-permute-start | bytes 196616 | tf_op jit(solution)/shard_map/while/body/eval_jaxpr/ppermute | solution.py:12
  284.7 7.7 %collective-permute-start.1 = (bf16[64,512]{1,0:T(8,128)(2,1)S(1)}, bf16[64,512]{1,0:T(8,128)(2,1)S(1)}, u32[]{:S(2)}, u32[]{:S(2)}) collective-permute-start(bf16[64,512]{1,0:T(8,128)(2,1)S(1)} %copy.151), channel_id=1, source_target_pairs={{0,16},{16,32},{32,48},{48,64},{64,80},{80,96},{96,112},{112,128},... | collective-permute-start | bytes 196616 | tf_op jit(solution)/shard_map/while/body/eval_jaxpr/ppermute | solution.py:12
  286.6 5.8 %collective-permute-start.2 = (bf16[64,512]{1,0:T(8,128)(2,1)S(1)}, bf16[64,512]{1,0:T(8,128)(2,1)S(1)}, u32[]{:S(2)}, u32[]{:S(2)}) collective-permute-start(bf16[64,512]{1,0:T(8,128)(2,1)S(1)} %fusion.162), channel_id=1, source_target_pairs={{0,16},{16,32},{32,48},{48,64},{64,80},{80,96},{96,112},{112,128},... | collective-permute-start | bytes 196616 | tf_op jit(solution)/shard_map/while/body/eval_jaxpr/ppermute | solution.py:12
  292.4 8.8 %collective-permute-start.1 = (bf16[64,512]{1,0:T(8,128)(2,1)S(1)}, bf16[64,512]{1,0:T(8,128)(2,1)S(1)}, u32[]{:S(2)}, u32[]{:S(2)}) collective-permute-start(bf16[64,512]{1,0:T(8,128)(2,1)S(1)} %copy.151), channel_id=1, source_target_pairs={{0,16},{16,32},{32,48},{48,64},{64,80},{80,96},{96,112},{112,128},... | collective-permute-start | bytes 196616 | tf_op jit(solution)/shard_map/while/body/eval_jaxpr/ppermute | solution.py:12
  294.3 6.9 %collective-permute-start.2 = (bf16[64,512]{1,0:T(8,128)(2,1)S(1)}, bf16[64,512]{1,0:T(8,128)(2,1)S(1)}, u32[]{:S(2)}, u32[]{:S(2)}) collective-permute-start(bf16[64,512]{1,0:T(8,128)(2,1)S(1)} %fusion.162), channel_id=1, source_target_pairs={{0,16},{16,32},{32,48},{48,64},{64,80},{80,96},{96,112},{112,128},... | collective-permute-start | bytes 196616 | tf_op jit(solution)/shard_map/while/body/eval_jaxpr/ppermute | solution.py:12
  302.9 49.7 %copy-start.11 = (bf16[64,4,512]{2,1,0:T(4,128)(2,1)S(1)}, bf16[64,4,512]{2,1,0:T(4,128)(2,1)}, u32[]{:S(2)}) copy-start(bf16[64,4,512]{2,1,0:T(4,128)(2,1)} %param.16) | copy-start | bytes 786436
  304.4 37.5 %all-to-all-start.3 = ((bf16[16,1,2]{2,1,0:T(2,128)(2,1)}), bf16[16,1,2]{2,1,0:T(2,128)(2,1)S(1)}, u32[]{:S(2)}, u32[]{:S(2)}) async-start(bf16[16,1,2]{2,1,0:T(2,128)(2,1)} %copy.81), calls=%async_computation.4 | async-start | bytes 16384 | tf_op jit(solution)/shard_map/all_to_all | solution.py:161
  318.8 39.6 %copy-start.16 = (s32[128,8]{0,1:T(8,128)S(1)}, s32[128,8]{0,1:T(8,128)}, u32[]{:S(2)}) copy-start(s32[128,8]{0,1:T(8,128)} %param.23) | copy-start | bytes 12292
  341.9 15.8 %copy-start.17 = (bf16[16,1,2]{2,1,0:T(2,128)(2,1)}, bf16[16,1,2]{2,1,0:T(2,128)(2,1)S(1)}, u32[]{:S(2)}) copy-start(bf16[16,1,2]{2,1,0:T(2,128)(2,1)S(1)} %all-to-all-done.3) | copy-start | bytes 196
  341.9 172.6 %all-to-all-start.2 = ((bf16[16,1,2,7168]{3,2,1,0:T(2,128)(2,1)}), bf16[16,1,2,7168]{3,2,1,0:T(2,128)(2,1)S(1)}, u32[]{:S(2)}, u32[]{:S(2)}) async-start(bf16[16,1,2,7168]{3,2,1,0:T(2,128)(2,1)} %copy.79), calls=%async_computation.3 | async-start | bytes 917504 | tf_op jit(solution)/shard_map/all_to_all | solution.py:160
  352.5 160.3 %all-reduce.3.cloned.1.call-start = ((), (), s32[]{:S(2)}) async-start(), calls=%async_computation.6 | async-start | bytes 131072 | tf_op jit(solution)/shard_map/psum | solution.py:107
  352.8 4.9 collective-permute-start.3
  (9 other events, 27.4 us)
Sparse Core Ops, SparseCore 0:
  42.4 49.7 all-gather.6
  94.1 54.8 all-gather.4
  176.0 62.4 reduce-scatter.6
  240.9 98.7 reduce-scatter.4
Sparse Core Ops, SparseCore 1:
  358.5 154.3 all-reduce.2
where the time goes:
time: 527 us; the launch traced here: 525 us
  waiting for transfers between devices  309 us (59%)
  matrix products  71.4 us (14%)
  starting transfers between devices  39.8 us (8%)
  local copies, waits for them, and re-layouts  39.7 us (8%)
  blocking collectives  39.5 us (7%)
  between operations  16.3 us (3%)
  other arithmetic  6.69 us (1%)
    psum x1, waiting for transfers between devices, attention_grads(): d_latent = lax.psum(own_latent.astype(jnp.bfloat16), 'exp')  154 us
    ppermute x46, waiting for transfers between devices, passed_along(): lax.ppermute(array, axis, [(i, (i + by) % count) for i in range(count)])  134 us
    all_to_all x1, blocking collectives, expert_grads(): lax.all_to_all(send_in, 'exp', split_axis=0, concat_axis=0, tiled=True)  28.4 us
    dynamic_slice x31, local copies, waits for them, and re-layouts, masked_scores(): key_docs = lax.dynamic_slice_in_dim(all_docs, source * row_count, row_count)  23.4 us
    reduce_scatter x1, waiting for transfers between devices, expert_grads(): lax.psum_scatter((term + jnp.einsum('nech,edh->necd', up_grad, w_up, pref...  20.8 us
    all_to_all x1, starting transfers between devices, expert_grads(): lax.all_to_all(score_sums.astype(jnp.bfloat16), 'exp', split_axis=0, conc...  14.4 us
    unnamed x1, blocking collectives  11.2 us
    dot_general x1, matrix products, expert_grads(): jnp.einsum('nech,edh->necd', up_grad, w_up, preferred_element_type=jnp.fl...  10.8 us
  transfers between devices with their start and end apart: 54, of which 34 were waited for; matrix products, arithmetic and copies ran while one was open for 18% of the time, Pallas kernels for 0%

commit v1 on v0

v1 whole, which is shorter than its diff:
```python
import functools

import jax
import jax.numpy as jnp
from jax import lax
from jax.experimental import pallas as pl
from jax.experimental.pallas import tpu as pltpu
from jax.sharding import PartitionSpec as P

SCALE = 192 ** (-0.5)
CAP = 2
MESH = pl.DeviceIdType.MESH
BF = jnp.bfloat16
F32 = jnp.float32

N_X, N_Y, N_CORE = 4, 2, 2
N_CTX, N_EXP = 16, 16
CHIPS = N_X * N_Y
D = 7168
HALF = D // 2
SHARD = 128
HID2 = 2 * SHARD
LAT = 512
KW = LAT + 128
T_ATT = 64
ROWS_ATT = 256
BLK = 64
OUTW = HALF + 128


def nt(a, b):
    return lax.dot_general(a, b, (((1,), (1,)), ((), ())), preferred_element_type=F32)


def nn(a, b):
    return lax.dot_general(a, b, (((1,), (0,)), ((), ())), preferred_element_type=F32)


def tn(a, b):
    return lax.dot_general(a, b, (((0,), (0,)), ((), ())), preferred_element_type=F32)


def kernel(
    sin_ref,
    sgr_ref,
    wg_hbm,
    wu_hbm,
    wd_hbm,
    kext_ref,
    q_ref,
    do_ref,
    qdoc_ref,
    back_ref,
    dq_ref,
    dlat_ref,
    ra,
    xg,
    wg,
    wu,
    wd,
    pbuf,
    prec,
    ggb,
    ugb,
    parts,
    rsb,
    bsend,
    kbuf,
    dsb,
    pwb,
    dkf,
    dkb,
    drec,
    s2b,
    rbuf,
    e1,
    ebuf,
    f1,
    dlat,
    sem_l,
    sem_as,
    sem_ar,
    sem_ks,
    sem_kr,
    sem_ws,
    sem_wr,
    sem_gs,
    sem_gr,
    sem_ps,
    sem_pr,
    sem_rs,
    sem_rr,
    sem_bs,
    sem_br,
    sem_ds,
    sem_dr,
):
    c = lax.axis_index("ctx")
    e = lax.axis_index("exp")
    core = lax.rem(c, 2)
    chip = lax.div(c, 2)
    y = lax.rem(chip, 2)
    x = lax.div(chip, 2)
    sib = c + 1 - 2 * core
    other = 1 - core

    def at(ctx, exp):
        return {"ctx": ctx, "exp": exp}

    def remote(src, dst, ssem, rsem, ctx, exp):
        return pltpu.make_async_remote_copy(
            src_ref=src,
            dst_ref=dst,
            send_sem=ssem,
            recv_sem=rsem,
            device_id=at(ctx, exp),
            device_id_type=MESH,
        )

    def take(ref, sem):
        pltpu.make_async_copy(ref, ref, sem).wait()

    def chip_at(r):
        return lax.rem(chip + r, CHIPS)

    lane0 = pl.multiple_of(core * SHARD, SHARD)
    own_d = pl.ds(pl.multiple_of(core * HALF, HALF), HALF)
    oth_d = pl.ds(pl.multiple_of(other * HALF, HALF), HALF)
    loc = [
        pltpu.make_async_copy(wg_hbm.at[own_d, :], wg.at[:, pl.ds(lane0, SHARD)], sem_l.at[0]),
        pltpu.make_async_copy(wu_hbm.at[own_d, :], wu.at[:, pl.ds(lane0, SHARD)], sem_l.at[1]),
        pltpu.make_async_copy(wd_hbm.at[:, own_d], wd.at[pl.ds(lane0, SHARD), :], sem_l.at[2]),
    ]
    for cp in loc:
        cp.start()

    bar = pltpu.get_barrier_semaphore()
    for r in range(CHIPS):
        for k in range(N_CORE):
            if r or k:
                to = 2 * chip_at(r) + lax.rem(core + k, 2)
                pl.semaphore_signal(bar, inc=1, device_id=at(to, e), device_id_type=MESH)
    for i in range(1, N_EXP):
        for k in range(N_CORE):
            to = 2 * chip + lax.rem(core + k, 2)
            pl.semaphore_signal(
                bar, inc=1, device_id=at(to, lax.rem(e + i, N_EXP)), device_id_type=MESH
            )
    pl.semaphore_wait(bar, 15 + 30)

    for arr, ref in enumerate((sin_ref, sgr_ref)):
        for i in range(N_EXP):
            te = lax.rem(e + i, N_EXP)
            for k in range(N_CORE):
                tc = lax.rem(core + k, 2)
                src = ref.at[te, :, pl.ds(pl.multiple_of(tc * HALF, HALF), HALF)]
                dst = ra.at[arr, core * N_EXP + e]
                if i == 0 and k == 0:
                    pltpu.make_async_copy(src, dst, sem_l.at[3 + arr]).start()
                else:
                    remote(src, dst, sem_as.at[arr], sem_ar.at[arr], 2 * chip + tc, te).start()

    for r in range(CHIPS):
        for k in range(N_CORE):
            row = (2 * ((CHIPS - r) % CHIPS) + core) * T_ATT
            dst = kbuf.at[pl.ds(pl.multiple_of(row, T_ATT), T_ATT), :]
            if r == 0 and k == 0:
                pltpu.make_async_copy(kext_ref, dst, sem_l.at[5]).start()
            else:
                to = 2 * chip_at(r) + lax.rem(core + k, 2)
                remote(kext_ref, dst, sem_ks, sem_kr, to, e).start()

    rem = [
        remote(wg_hbm.at[oth_d, :], wg.at[:, pl.ds(lane0, SHARD)], sem_ws.at[0], sem_wr.at[0], sib, e),
        remote(wu_hbm.at[oth_d, :], wu.at[:, pl.ds(lane0, SHARD)], sem_ws.at[1], sem_wr.at[1], sib, e),
        remote(wd_hbm.at[:, oth_d], wd.at[pl.ds(lane0, SHARD), :], sem_ws.at[2], sem_wr.at[2], sib, e),
    ]
    for cp in rem:
        cp.start()

    right = 4 * lax.rem(x + 1, N_X) + 2 * y + core
    left = 4 * lax.rem(x + 3, N_X) + 2 * y + core
    mate = 4 * x + 2 * (1 - y) + core

    hops = {}

    def hop(name, index, arr, dx, dy, way, lo=0, n=BLK):
        if way == "R":
            to, tx, ty = right, (dx + 3) % 4, dy
        elif way == "L":
            to, tx, ty = left, (dx + 1) % 4, dy
        else:
            to, tx, ty = mate, dx, 1 - dy
        hops[name] = remote(
            xg.at[arr, dx, pl.ds(dy * BLK + lo, n), :],
            xg.at[arr, tx, pl.ds(ty * BLK + lo, n), :],
            sem_gs.at[index],
            sem_gr.at[index],
            to,
            e,
        )
        hops[name].start()

    def got(*names):
        for name in names:
            hops[name].wait_recv()

    def repack(arr):
        pltpu.make_async_copy(
            sin_ref.at[0, :, pl.ds(0, HALF)], ra.at[arr, 0], sem_l.at[3 + arr]
        ).wait()
        take(ra.at[arr, pl.ds(0, 31)], sem_ar.at[arr])

        def body(t, carry):
            lanes = pl.ds(pl.multiple_of(t * 512, 512), 512)
            for g in range(4):
                rows = [ra[arr, 8 * g + i, :, lanes].astype(F32) for i in range(8)]
                xg[arr, 0, pl.ds(16 * g, 16), lanes] = jnp.concatenate(rows, axis=0).astype(BF)
            return carry

        lax.fori_loop(0, HALF // 512, body, 0)

    repack(0)
    hop("TY", 0, 0, 0, 0, "Y")
    hop("TR", 1, 0, 0, 0, "R")
    hop("TL", 2, 0, 0, 0, "L")
    repack(1)
    hop("GR", 3, 1, 0, 0, "R")
    hop("GL", 4, 1, 0, 0, "L")
    hop("GY", 5, 1, 0, 0, "Y")

    pltpu.make_async_copy(kext_ref, kbuf.at[pl.ds(0, T_ATT), :], sem_l.at[5]).wait()
    take(kbuf.at[pl.ds(0, 15 * T_ATT), :], sem_kr)

    def att(h, carry):
        rows = pl.ds(pl.multiple_of(h * 64, 64), 64)
        keys = kbuf[:, :LAT]
        same = nt(qdoc_ref[rows, :], kbuf[:, LAT:])
        s = nt(q_ref[rows, :], keys) * SCALE
        s = jnp.where(same > 0.5, s, -1e30)
        m = jnp.max(s, axis=1, keepdims=True)
        p = jnp.exp(s - m)
        total = jnp.sum(p, axis=1, keepdims=True)
        dp = nt(do_ref[rows, :], keys)
        delta = jnp.sum(p.astype(BF).astype(F32) * dp, axis=1, keepdims=True) / total
        probs = p / total
        ds = (probs * (dp - delta)).astype(BF)
        dsb[rows, :] = ds
        pwb[rows, :] = probs.astype(BF)
        dq_ref[rows, :] = (nn(ds, keys) * SCALE).astype(BF)
        return carry

    lax.fori_loop(0, ROWS_ATT // 64, att, 0)

    def dkeys(k, carry):
        lanes = pl.ds(pl.multiple_of(k * 128, 128), 128)
        val = tn(dsb[:, lanes], q_ref[...]) * SCALE + tn(pwb[:, lanes], do_ref[...])
        dkf[k] = val
        dkb[0, k] = val[:64].astype(BF)
        dkb[1, k] = val[64:].astype(BF)
        return carry

    lax.fori_loop(0, CHIPS, dkeys, 0)
    dk_sib = remote(dkb.at[other], drec, sem_ds.at[0], sem_dr.at[0], sib, e)
    dk_sib.start()

    got("TY")
    hop("T1R", 6, 0, 0, 1, "R")
    hop("T1L", 7, 0, 0, 1, "L")
    got("GR", "GL")
    hop("GhR", 8, 1, 3, 0, "R", 0, 32)
    hop("GhL", 9, 1, 1, 0, "L", 32, 32)
    hop("GlY", 10, 1, 3, 0, "Y")
    hop("GrY", 11, 1, 1, 0, "Y")
    got("TR", "TL")
    hop("ThR", 12, 0, 3, 0, "R", 0, 32)
    hop("ThL", 13, 0, 1, 0, "L", 32, 32)

    dk_sib.wait_recv()
    mine = pl.ds(pl.multiple_of(core * 64, 64), 64)
    dk_rs = []
    for r in range(1, CHIPS):
        s2b[r] = (dkf[r, mine, :] + drec[r].astype(F32)).astype(BF)
        cp = remote(
            s2b.at[r],
            rbuf.at[CHIPS - r - 1],
            sem_ds.at[r],
            sem_dr.at[CHIPS - r],
            2 * chip_at(r) + core,
            e,
        )
        cp.start()
        dk_rs.append(cp)

    for cp in loc:
        cp.wait()
    for cp in rem:
        cp.wait_recv()

    swaps = {}

    def forward(dx):
        xt, xd = xg[0, dx], xg[1, dx]
        pbuf[dx, 0] = nn(xt, wg[...])
        pbuf[dx, 1] = nn(xt, wu[...])
        pbuf[dx, 2] = nt(xd, wd[...])
        swaps[dx] = remote(pbuf.at[dx], prec.at[dx], sem_ps.at[dx], sem_pr.at[dx], sib, e)
        swaps[dx].start()

    owed = []

    def backward(dx):
        swaps[dx].wait_recv()
        gate = pbuf[dx, 0] + prec[dx, 0]
        up = pbuf[dx, 1] + prec[dx, 1]
        act = pbuf[dx, 2] + prec[dx, 2]
        sig = 1.0 / (1.0 + jnp.exp(-gate))
        silu = gate * sig
        hid = (silu * up).astype(BF).astype(F32)
        score = jnp.sum(hid * act, axis=1, keepdims=True)
        hi = score.astype(BF).astype(F32)
        lane = lax.broadcasted_iota(jnp.int32, (128, 128), 1)
        extra = jnp.where(lane == 0, hi, jnp.where(lane == 1, score - hi, 0.0))
        parts[dx, :, pl.ds(HALF, 128)] = extra.astype(BF)
        ggb[...] = (act * up * sig * (1.0 + gate * (1.0 - sig))).astype(BF)
        ugb[...] = (act * silu).astype(BF)

        def body(t, carry):
            cols = pl.ds(pl.multiple_of(t * 512, 512), 512)
            val = nt(ggb[...], wg[cols, :]) + nt(ugb[...], wu[cols, :])
            parts[dx, :, cols] = val.astype(BF)
            return carry

        lax.fori_loop(0, HALF // 512, body, 0)
        for dy in range(2):
            if dx or dy:
                tx = (4 - dx) % 4
                index = 2 * dx + dy
                to = 4 * lax.rem(x + dx, N_X) + 2 * lax.rem(y + dy, 2) + core
                cp = remote(
                    parts.at[dx, pl.ds(dy * BLK, BLK), :],
                    rsb.at[tx, pl.ds(dy * BLK, BLK), :],
                    sem_rs.at[index],
                    sem_rr.at[2 * tx + dy],
                    to,
                    e,
                )
                cp.start()
                owed.append((2 * tx + dy, cp))

    got("GY")
    forward(0)
    got("GhR", "GhL")
    hop("Gh0Y", 14, 1, 2, 0, "Y", 0, 32)
    hop("Gh1Y", 15, 1, 2, 0, "Y", 32, 32)
    got("T1R", "T1L")
    hop("T1hR", 16, 0, 3, 1, "R", 0, 32)
    hop("T1hL", 17, 0, 1, 1, "L", 32, 32)
    backward(0)

    for cp in dk_rs:
        cp.wait_recv()
    tot = dkf[0, mine, :] + drec[0].astype(F32)
    for r in range(CHIPS - 1):
        tot = tot + rbuf[r].astype(F32)
    e1[...] = tot.astype(BF)

    def piece(i):
        return (
            pl.ds(pl.multiple_of(lax.div(i, 4) * 16, 16), 16),
            pl.ds(pl.multiple_of(lax.rem(i, 4) * 128, 128), 128),
        )

    rows_e, lanes_e = piece(e)
    own_piece = pltpu.make_async_copy(e1.at[rows_e, lanes_e], ebuf.at[15], sem_l.at[6])
    own_piece.start()
    for i in range(1, N_EXP):
        te = lax.rem(e + i, N_EXP)
        rows_t, lanes_t = piece(te)
        remote(e1.at[rows_t, lanes_t], ebuf.at[i - 1], sem_ds.at[8], sem_dr.at[8], c, te).start()

    got("GlY")
    forward(3)
    got("GrY")
    forward(1)
    backward(3)

    own_piece.wait()
    take(ebuf.at[pl.ds(0, 15)], sem_dr.at[8])
    tot = ebuf[0].astype(F32)
    for i in range(1, N_EXP):
        tot = tot + ebuf[i].astype(F32)
    f1[...] = tot.astype(BF)
    own_final = pltpu.make_async_copy(f1, dlat.at[rows_e, lanes_e], sem_l.at[7])
    own_final.start()
    for i in range(1, N_EXP):
        te = lax.rem(e + i, N_EXP)
        remote(f1, dlat.at[rows_e, lanes_e], sem_ds.at[9], sem_dr.at[9], c, te).start()

    backward(1)
    got("ThR", "ThL", "T1hR", "T1hL", "Gh0Y", "Gh1Y")
    forward(2)
    backward(2)

    own_final.wait()
    take(ebuf.at[pl.ds(0, 15)], sem_dr.at[9])
    dlat_ref[...] = dlat[...]

    for _, cp in owed:
        cp.wait_recv()

    def total(cols):
        val = parts[0, pl.ds(0, BLK), cols].astype(F32)
        for index in range(1, 8):
            val = val + rsb[index // 2, pl.ds((index % 2) * BLK, BLK), cols].astype(F32)
        return val

    def spread(val, cols):
        for i in range(32):
            bsend[i, :, cols] = val[2 * i : 2 * i + 2, :]

    def body(t, carry):
        cols = pl.ds(pl.multiple_of(t * 256, 256), 256)
        spread(total(cols).astype(BF), cols)
        return carry

    lax.fori_loop(0, HALF // 256, body, 0)
    cols = pl.ds(HALF, 128)
    score = jnp.sum(total(cols), axis=1, keepdims=True)
    spread(jnp.broadcast_to(score, (BLK, 128)).astype(BF), cols)

    for i in range(N_EXP):
        te = lax.rem(e + i, N_EXP)
        for k in range(N_CORE):
            tc = lax.rem(core + k, 2)
            src = bsend.at[tc * N_EXP + te]
            dst = back_ref.at[core * N_EXP + e]
            if i == 0 and k == 0:
                pltpu.make_async_copy(src, dst, sem_l.at[8]).start()
            else:
                remote(src, dst, sem_bs, sem_br, 2 * chip + tc, te).start()

    take(ra.at[0, pl.ds(0, 31)], sem_as.at[0])
    take(ra.at[1, pl.ds(0, 31)], sem_as.at[1])
    take(kbuf.at[pl.ds(0, 15 * T_ATT), :], sem_ks)
    for cp in rem:
        cp.wait_send()
    for cp in hops.values():
        cp.wait_send()
    for cp in swaps.values():
        cp.wait_send()
    for _, cp in owed:
        cp.wait_send()
    dk_sib.wait_send()
    for cp in dk_rs:
        cp.wait_send()
    take(ebuf.at[pl.ds(0, 15)], sem_ds.at[8])
    take(ebuf.at[pl.ds(0, 15)], sem_ds.at[9])
    take(bsend.at[pl.ds(0, 31)], sem_bs)
    pltpu.make_async_copy(bsend.at[0], back_ref.at[0], sem_l.at[8]).wait()
    take(bsend.at[pl.ds(0, 31)], sem_br)


def fused(sin, sgr, wg, wu, wd, kext, q, do, qdoc):
    vmem = pl.BlockSpec(memory_space=pltpu.VMEM)
    hbm = pl.BlockSpec(memory_space=pl.ANY)
    dma = pltpu.SemaphoreType.DMA
    return pl.pallas_call(
        kernel,
        out_shape=(
            jax.ShapeDtypeStruct((32, 2, OUTW), BF),
            jax.ShapeDtypeStruct((ROWS_ATT, LAT), BF),
            jax.ShapeDtypeStruct((T_ATT, LAT), BF),
        ),
        in_specs=[hbm] * 5 + [vmem] * 4,
        out_specs=(vmem, vmem, vmem),
        scratch_shapes=[
            pltpu.VMEM((2, 32, 2, HALF), BF),
            pltpu.VMEM((2, N_X, 2 * BLK, HALF), BF),
            pltpu.VMEM((HALF, HID2), BF),
            pltpu.VMEM((HALF, HID2), BF),
            pltpu.VMEM((HID2, HALF), BF),
            pltpu.VMEM((N_X, 3, 2 * BLK, HID2), F32),
            pltpu.VMEM((N_X, 3, 2 * BLK, HID2), F32),
            pltpu.VMEM((2 * BLK, HID2), BF),
            pltpu.VMEM((2 * BLK, HID2), BF),
            pltpu.VMEM((N_X, 2 * BLK, OUTW), BF),
            pltpu.VMEM((N_X, 2 * BLK, OUTW), BF),
            pltpu.VMEM((32, 2, OUTW), BF),
            pltpu.VMEM((16 * T_ATT, KW), BF),
            pltpu.VMEM((ROWS_ATT, 16 * T_ATT), BF),
            pltpu.VMEM((ROWS_ATT, 16 * T_ATT), BF),
            pltpu.VMEM((CHIPS, 128, LAT), F32),
            pltpu.VMEM((2, CHIPS, 64, LAT), BF),
            pltpu.VMEM((CHIPS, 64, LAT), BF),
            pltpu.VMEM((CHIPS, 64, LAT), BF),
            pltpu.VMEM((CHIPS - 1, 64, LAT), BF),
            pltpu.VMEM((T_ATT, LAT), BF),
            pltpu.VMEM((16, 16, 128), BF),
            pltpu.VMEM((16, 128), BF),
            pltpu.VMEM((T_ATT, LAT), BF),
            dma((9,)),
            dma((2,)),
            dma((2,)),
            dma,
            dma,
            dma((3,)),
            dma((3,)),
            dma((18,)),
            dma((18,)),
            dma((4,)),
            dma((4,)),
            dma((8,)),
            dma((8,)),
            dma,
            dma,
            dma((10,)),
            dma((10,)),
        ],
        compiler_params=pltpu.CompilerParams(
            collective_id=0, has_side_effects=True, vmem_limit_bytes=60 * 1024 * 1024
        ),
        name="fused",
    )(sin, sgr, wg, wu, wd, kext, q, do, qdoc)


def local(
    queries,
    latent,
    grad_out,
    doc_ids,
    tokens,
    token_grads,
    gate_values,
    expert_ids,
    gate_order,
    w_gate,
    w_up,
    w_down,
):
    docs = jnp.arange(128, dtype=jnp.int32)
    onehot = (doc_ids[:, None] == docs).astype(BF)
    kext = jnp.concatenate([latent, onehot], axis=1)
    heads = queries.shape[1]
    qdoc = jnp.repeat(onehot, heads, axis=0)
    q = queries.reshape(ROWS_ATT, LAT)
    do = grad_out.reshape(ROWS_ATT, LAT)

    span = jnp.arange(N_EXP, dtype=jnp.int32)
    matches = (expert_ids[:, :, None] == span).astype(jnp.int32)
    hits = jnp.sum(matches, axis=1)
    priority = gate_order[0]
    earlier = (priority[:, None] < priority[None, :]).astype(jnp.int32)
    ranks = jnp.einsum("ut,ue->te", earlier, hits)
    chosen = (hits[:, :, None] == 1) & (ranks[:, :, None] == jnp.arange(CAP, dtype=jnp.int32))
    picker = chosen.astype(BF)
    sin = jnp.einsum("tes,td->esd", picker, tokens, preferred_element_type=F32).astype(BF)
    sgr = jnp.einsum("tes,td->esd", picker, token_grads, preferred_element_type=F32).astype(BF)

    back, dq, dlat = fused(
        sin, sgr, w_gate[0], w_up[0], w_down[0], kext, q, do, qdoc
    )

    rows = back.reshape(2, N_EXP, CAP, OUTW)
    gate_mass = jnp.sum(matches.astype(F32) * gate_values[:, :, None], axis=1)
    weighting = chosen.astype(F32) * gate_mass[:, :, None]
    d_tokens = jnp.einsum(
        "tes,hesd->thd",
        weighting,
        rows[..., :HALF].astype(F32),
        precision=lax.Precision.HIGHEST,
    ).reshape(tokens.shape)
    kept = jnp.einsum(
        "tes,es->te",
        chosen.astype(F32),
        rows[0, :, :, HALF].astype(F32),
        precision=lax.Precision.HIGHEST,
    )
    d_gates = jnp.einsum(
        "tke,te->tk", matches.astype(F32), kept, precision=lax.Precision.HIGHEST
    )
    return (dq.reshape(queries.shape), dlat, d_tokens.astype(BF), d_gates.astype(BF))


def solution(mesh):
    in_specs = (
        P("ctx", "exp", None),
        P("ctx", None),
        P("ctx", "exp", None),
        P("ctx"),
        P(("ctx", "exp"), None),
        P(("ctx", "exp"), None),
        P(("ctx", "exp"), None),
        P(("ctx", "exp"), None),
        P(("ctx", "exp"), None),
        P("exp", None, "ctx"),
        P("exp", None, "ctx"),
        P("exp", "ctx", None),
    )
    out_specs = (
        P("ctx", "exp", None),
        P("ctx", None),
        P(("ctx", "exp"), None),
        P(("ctx", "exp"), None),
    )
    return jax.shard_map(local, mesh=mesh, in_specs=in_specs, out_specs=out_specs, check_vma=False)
```

time: 527 us -> 220 us (0.42)
  the two profiles are of different devices: /device:TPU:2 before, /device:TPU:1 now
where the time goes in v1:
time: 220 us; the launch traced here: 219 us
  Pallas kernels  190 us (86%)
  local copies, waits for them, and re-layouts  18.9 us (9%)
  matrix products  4.67 us (2%)
  other arithmetic  4.39 us (2%)
    pallas_call x1, Pallas kernels, fused(): pl.pallas_call(kernel, out_shape=(jax.ShapeDtypeStruct((32, 2, OUTW), BF)...  190 us
    unnamed x11, local copies, waits for them, and re-layouts  4.66 us

profile of v1, /device:TPU:1, one launch (start us, length us, event | category | flops | bytes accessed | tf_op | source)
XLA Modules:
  0.0 219.1 jit_solution(5934785609654215472)
XLA Ops:
  0.6 0.0 copy-start
  0.6 0.8 convert_reduce_fusion
  1.5 0.9 fusion.11
  2.5 0.7 fusion.8
  3.2 0.7 fusion.15
  3.9 0.7 broadcast_in_dim.2
  4.6 1.5 pad_maximum_fusion.kext_ref
  6.0 1.7 reshape.35.q_ref
  7.8 1.7 reshape.36.do_ref
  9.5 0.0 copy-done
  9.5 0.0 copy-start.1
  9.5 0.4 fusion.1
  9.9 1.3 copy.54.sgr_ref
  11.1 0.0 copy-done.1
  11.1 0.4 fusion.3
  11.5 1.2 copy.55.sin_ref
  12.7 0.0 copy-start.3
  12.7 190.4 %fused.1 = (bf16[32,2,3712]{2,1,0:T(2,128)(2,1)}, bf16[256,512]{1,0:T(8,128)(2,1)}, bf16[64,512]{1,0:T(8,128)(2,1)}) custom-call(bf16[16,2,7168]{2,1,0:T(2,128)(2,1)} %copy.55.sin_ref, bf16[16,2,7168]{2,1,0:T(2,128)(2,1)} %copy.54.sgr_ref, bf16[7168,128]{1,0:T(8,128)(2,1)} %bitcast.39, bf16[7168,128]{1,0:T(8,128)(2,1)} %bitcast.40, ...), custom_call_target="tpu_custom_call" | custom-call | tf_op jit(solution)/shard_map/fused/pallas_call | solution.py:468
  203.2 1.7 reshape.38
  204.9 0.7 slice.9
  205.6 1.3 slice.8
  206.9 0.1 copy.46
  207.0 0.1 copy.37
  207.2 0.1 fusion.16
  207.3 0.0 copy-done.3
  207.3 0.6 fusion.10
  207.9 2.9 %fusion = bf16[128,2,3584]{2,0,1:T(8,128)(2,1)} fusion(bf16[2,16,2,3584]{3,2,1,0:T(2,128)(2,1)S(1)} %slice.8, pred[128,16,2]{0,1,2:T(8,128)(4,1)S(1)} %fusion.20, f32[128,16]{0,1:T(8,128)S(1)} %fusion.8), kind=kOutput, calls=%fused_computation.1 | convolution fusion | flops 353243136 | bytes 2306048 | tf_op jit(solution)/shard_map/tes,hesd->thd/dot_general | solution.py:567
  210.8 3.8 %copy.33 = bf16[128,2,3584]{0,2,1:T(8,128)(2,1)} copy(bf16[128,2,3584]{2,0,1:T(8,128)(2,1)} %fusion) | data formatting | bytes 3670016 | tf_op jit(solution)/shard_map/convert_element_type | solution.py:582
  214.6 0.0 copy-start.2
  214.6 3.9 %copy.35 = bf16[128,7168]{1,0:T(8,128)(2,1)} copy(bf16[128,7168]{0,1:T(8,128)(2,1)} %bitcast.38) | data formatting | bytes 3670016
  218.5 0.0 copy-done.2
  218.5 0.6 copy.57
  (2 shorter events, 0.0 us)
Async XLA Ops:
  0.6 8.9 %copy-start = (bf16[128,7168]{1,0:T(8,128)(2,1)S(1)}, bf16[128,7168]{1,0:T(8,128)(2,1)}, u32[]{:S(2)}) copy-start(bf16[128,7168]{1,0:T(8,128)(2,1)} %param.17) | copy-start | bytes 5505028
  9.5 1.6 copy-start.1
  12.7 194.6 %copy-start.3 = (s32[128,8]{0,1:T(8,128)S(1)}, s32[128,8]{0,1:T(8,128)}, u32[]{:S(2)}) copy-start(s32[128,8]{0,1:T(8,128)} %param.19) | copy-start | bytes 12292
  214.6 3.9 %copy-start.2 = (bf16[64,512]{1,0:T(8,128)(2,1)S(1)}, bf16[64,512]{1,0:T(8,128)(2,1)}, u32[]{:S(2)}) copy-start(bf16[64,512]{1,0:T(8,128)(2,1)} %get-tuple-element.23) | copy-start | bytes 196612

commit v2 on v1

v2 whole, which is shorter than its diff:
```python
import jax
import jax.numpy as jnp
from jax import lax
from jax.experimental import pallas as pl
from jax.experimental.pallas import tpu as pltpu
from jax.sharding import PartitionSpec as P

SCALE = 192 ** (-0.5)
MESH = pl.DeviceIdType.MESH
BF = jnp.bfloat16
F32 = jnp.float32

N_X, N_CORE = 4, 2
N_EXP = 16
CHIPS = 8
D = 7168
HALF = D // 2
SHARD = 128
HID2 = 2 * SHARD
LAT = 512
KW = LAT + 128
T_ATT = 64
ROWS_ATT = 256
BLK = 64
PAIRS = 32
EXTRA = 128
OUTW = EXTRA + HALF
STEP = 256
COLS = ((0, EXTRA + HALF // 2), (EXTRA + HALF // 2, HALF // 2))


def nt(a, b):
    return lax.dot_general(a, b, (((1,), (1,)), ((), ())), preferred_element_type=F32)


def nn(a, b):
    return lax.dot_general(a, b, (((1,), (0,)), ((), ())), preferred_element_type=F32)


def tn(a, b):
    return lax.dot_general(a, b, (((0,), (0,)), ((), ())), preferred_element_type=F32)


def route(ids, prio):
    pair = lax.broadcasted_iota(jnp.int32, (PAIRS, 128), 0)
    expert = lax.shift_right_logical(pair, 1)
    slot = (pair - 2 * expert).astype(F32)
    hits = jnp.zeros((PAIRS, 128), F32)
    for k in range(8):
        hits = hits + jnp.where(ids[k : k + 1, :] == expert, 1.0, 0.0)
    later = jnp.broadcast_to(prio.astype(F32), (128, 128))
    earlier = jnp.where(later.T < later, 1.0, 0.0)
    ranks = nn(hits.astype(BF), earlier.astype(BF))
    chosen = jnp.where((hits == 1.0) & (ranks == slot), 1.0, 0.0)
    return chosen, expert


def split_score(score):
    hi = score.astype(BF).astype(F32)
    lane = lax.broadcasted_iota(jnp.int32, (score.shape[0], EXTRA), 1)
    return jnp.where(lane == 0, hi, jnp.where(lane == 1, score - hi, 0.0)).astype(BF)


def kernel(
    ids_ref, prio_ref, docs_ref, tok_hbm, grd_hbm, wg_hbm, wu_hbm, wd_hbm, lat_hbm, q_hbm, do_hbm,
    back_ref, dq_ref, dlat_ref,
    rows_v, snd, ra, xg, wg, wu, wd, pbuf, prec, ggb, ugb, parts, rsx, rsm, s2p, rsf, rs2, ysend, rsy, bsend,
    q3, do3, qs, dos, qd, dqs, kbuf, dsb, pwb, dkf, dkb, drec, s2b, ebuf, e8, rbuf, f1, dlat,
    sem_l, sem_as, sem_ar, sem_ks, sem_kr, sem_ws, sem_wr, sem_gs, sem_gr, sem_ps, sem_pr,
    sem_rs, sem_rr, sem_bs, sem_br, sem_ds, sem_dr,
):
    c = lax.axis_index("ctx")
    e = lax.axis_index("exp")
    core = lax.rem(c, 2)
    chip = lax.div(c, 2)
    y = lax.rem(chip, 2)
    x = lax.div(chip, 2)
    sib = c + 1 - 2 * core
    other = 1 - core
    right = 4 * lax.rem(x + 1, N_X) + 2 * y + core
    left = 4 * lax.rem(x + 3, N_X) + 2 * y + core
    mate = 4 * x + 2 * (1 - y) + core

    def at(ctx, exp):
        return {"ctx": ctx, "exp": exp}

    def remote(src, dst, ssem, rsem, ctx, exp):
        return pltpu.make_async_remote_copy(
            src_ref=src,
            dst_ref=dst,
            send_sem=ssem,
            recv_sem=rsem,
            device_id=at(ctx, exp),
            device_id_type=MESH,
        )

    def take(ref, sem):
        pltpu.make_async_copy(ref, ref, sem).wait()

    def chip_at(r):
        return 2 * lax.rem(chip + r, CHIPS) + core

    lane0 = pl.multiple_of(core * SHARD, SHARD)
    own_d = pl.ds(pl.multiple_of(core * HALF, HALF), HALF)
    oth_d = pl.ds(pl.multiple_of(other * HALF, HALF), HALF)
    own_k = pl.ds(pl.multiple_of(core * 512, 512), 512)
    oth_k = pl.ds(pl.multiple_of(other * 512, 512), 512)
    own_b = pl.ds(pl.multiple_of(core * 512, 512), T_ATT)
    rows_in = [
        pltpu.make_async_copy(tok_hbm, rows_v.at[0], sem_l.at[0]),
        pltpu.make_async_copy(grd_hbm, rows_v.at[1], sem_l.at[1]),
    ]
    lat_in = pltpu.make_async_copy(lat_hbm, kbuf.at[own_b, pl.ds(0, LAT)], sem_l.at[2])
    att_in = [
        pltpu.make_async_copy(q_hbm, q3, sem_l.at[3]),
        pltpu.make_async_copy(do_hbm, do3, sem_l.at[4]),
    ]
    w_in = [
        pltpu.make_async_copy(wg_hbm.at[own_d, :], wg.at[:, pl.ds(lane0, SHARD)], sem_l.at[5]),
        pltpu.make_async_copy(wu_hbm.at[own_d, :], wu.at[:, pl.ds(lane0, SHARD)], sem_l.at[6]),
        pltpu.make_async_copy(wd_hbm.at[:, own_d], wd.at[pl.ds(lane0, SHARD), :], sem_l.at[7]),
    ]
    rows_in[0].start()
    lat_in.start()
    rows_in[1].start()

    bar = pltpu.get_barrier_semaphore()
    pl.semaphore_signal(bar, inc=1, device_id=at(sib, e), device_id_type=MESH)
    for r in range(1, CHIPS):
        pl.semaphore_signal(bar, inc=1, device_id=at(chip_at(r), e), device_id_type=MESH)
    for i in range(1, N_EXP):
        for k in range(N_CORE):
            to = at(2 * chip + lax.rem(core + k, 2), lax.rem(e + i, N_EXP))
            pl.semaphore_signal(bar, inc=1, device_id=to, device_id_type=MESH)
    for cp in att_in + w_in:
        cp.start()

    chosen, _ = route(ids_ref[...], prio_ref[...])
    picker = chosen.astype(BF)

    def pick(arr):
        rows_in[arr].wait()

        def body(t, carry):
            cols = pl.ds(pl.multiple_of(t * 512, 512), 512)
            val = nn(picker, rows_v[arr, :, cols]).astype(BF)
            snd[arr, :, :, cols] = val.reshape(N_EXP, 2, 512)
            return carry

        lax.fori_loop(0, D // 512, body, 0)

    def scatter(arr):
        for i in range(N_EXP):
            te = lax.rem(e + i, N_EXP)
            for k in range(N_CORE):
                tc = lax.rem(core + k, 2)
                src = snd.at[arr, te, :, pl.ds(pl.multiple_of(tc * HALF, HALF), HALF)]
                dst = ra.at[arr, core * N_EXP + e]
                if i == 0 and k == 0:
                    pltpu.make_async_copy(src, dst, sem_l.at[8 + arr]).start()
                else:
                    remote(src, dst, sem_as.at[arr], sem_ar.at[arr], 2 * chip + tc, te).start()

    pick(0)
    doc = lax.broadcasted_iota(jnp.int32, (128, T_ATT), 0)
    onehot_t = jnp.where(docs_ref[...] == doc, 1.0, 0.0).astype(BF)
    eye = jnp.where(
        lax.broadcasted_iota(jnp.int32, (128, 128), 0) == lax.broadcasted_iota(jnp.int32, (128, 128), 1),
        1.0,
        0.0,
    ).astype(BF)
    onehot = tn(onehot_t, eye).astype(BF)
    kbuf[own_b, pl.ds(LAT, 128)] = onehot
    lat_in.wait()

    pl.semaphore_wait(bar, 1 + 7 + 30)

    for r in range(1, CHIPS):
        row = core * 512 + (CHIPS - r) * T_ATT
        dst = kbuf.at[pl.ds(pl.multiple_of(row, T_ATT), T_ATT), :]
        remote(kbuf.at[own_b, :], dst, sem_ks.at[0], sem_kr.at[0], chip_at(r), e).start()
    scatter(0)
    pick(1)
    scatter(1)
    rem = [
        remote(wg_hbm.at[oth_d, :], wg.at[:, pl.ds(lane0, SHARD)], sem_ws.at[0], sem_wr.at[0], sib, e),
        remote(wu_hbm.at[oth_d, :], wu.at[:, pl.ds(lane0, SHARD)], sem_ws.at[1], sem_wr.at[1], sib, e),
        remote(wd_hbm.at[:, oth_d], wd.at[pl.ds(lane0, SHARD), :], sem_ws.at[2], sem_wr.at[2], sib, e),
    ]
    for cp in rem:
        cp.start()

    for cp in att_in:
        cp.wait()
    qs[...] = q3[...].reshape(ROWS_ATT, LAT)
    dos[...] = do3[...].reshape(ROWS_ATT, LAT)
    row_q = lax.shift_right_logical(lax.broadcasted_iota(jnp.int32, (ROWS_ATT, T_ATT), 0), 2)
    col_q = lax.broadcasted_iota(jnp.int32, (ROWS_ATT, T_ATT), 1)
    qd[...] = nn(jnp.where(row_q == col_q, 1.0, 0.0).astype(BF), onehot).astype(BF)

    take(kbuf.at[pl.ds(0, 7 * T_ATT), :], sem_kr.at[0])
    lat_sib = remote(kbuf.at[own_k, :], kbuf.at[own_k, :], sem_ks.at[1], sem_kr.at[1], sib, e)
    lat_sib.start()

    hops = {}

    def hop(name, index, arr, dx, dy, way, lo=0, n=BLK):
        if way == "R":
            to, tx, ty = right, (dx + 3) % 4, dy
        elif way == "L":
            to, tx, ty = left, (dx + 1) % 4, dy
        else:
            to, tx, ty = mate, dx, 1 - dy
        hops[name] = remote(
            xg.at[arr, dx, pl.ds(dy * BLK + lo, n), :],
            xg.at[arr, tx, pl.ds(ty * BLK + lo, n), :],
            sem_gs.at[index],
            sem_gr.at[index],
            to,
            e,
        )
        hops[name].start()

    def got(*names):
        for name in names:
            hops[name].wait_recv()

    def repack(arr):
        pltpu.make_async_copy(
            snd.at[0, 0, :, pl.ds(0, HALF)], ra.at[arr, 0], sem_l.at[8 + arr]
        ).wait()
        take(ra.at[arr, pl.ds(0, 31)], sem_ar.at[arr])

        def body(t, carry):
            cols = pl.ds(pl.multiple_of(t * 512, 512), 512)
            xg[arr, 0, pl.ds(0, BLK), cols] = ra[arr, :, :, cols].reshape(BLK, 512)
            return carry

        lax.fori_loop(0, HALF // 512, body, 0)

    repack(0)
    hop("TY", 0, 0, 0, 0, "Y")
    hop("TR", 1, 0, 0, 0, "R")
    hop("TL", 2, 0, 0, 0, "L")

    lat_sib.wait_recv()

    def att(h, carry):
        rows = pl.ds(pl.multiple_of(h * 64, 64), 64)
        keys = kbuf[:, :LAT]
        same = nt(qd[rows, :], kbuf[:, LAT:])
        s = nt(qs[rows, :], keys) * SCALE
        s = jnp.where(same > 0.5, s, -1e30)
        m = jnp.max(s, axis=1, keepdims=True)
        p = jnp.exp(s - m)
        total = jnp.sum(p, axis=1, keepdims=True)
        dp = nt(dos[rows, :], keys)
        delta = jnp.sum(p.astype(BF).astype(F32) * dp, axis=1, keepdims=True) / total
        probs = p / total
        ds = (probs * (dp - delta)).astype(BF)
        dsb[rows, :] = ds
        pwb[rows, :] = probs.astype(BF)
        dqs[rows, :] = (nn(ds, keys) * SCALE).astype(BF)
        return carry

    lax.fori_loop(0, ROWS_ATT // 64, att, 0)

    repack(1)
    hop("GR", 3, 1, 0, 0, "R")
    hop("GL", 4, 1, 0, 0, "L")
    hop("GY", 5, 1, 0, 0, "Y")
    got("TY")
    hop("T1R", 6, 0, 0, 1, "R")
    hop("T1L", 7, 0, 0, 1, "L")

    def dkeys(k, carry):
        rows = pl.ds(pl.multiple_of(k * 128, 128), 128)
        val = tn(dsb[:, rows], qs[...]) * SCALE + tn(pwb[:, rows], dos[...])
        dkf[rows, :] = val
        dkb[rows, :] = val.astype(BF)
        return carry

    lax.fori_loop(0, CHIPS, dkeys, 0)
    dk_sib = remote(dkb.at[oth_k, :], drec, sem_ds.at[0], sem_dr.at[0], sib, e)
    dk_sib.start()

    got("GR", "GL")
    hop("GhR", 8, 1, 3, 0, "R", 0, 32)
    hop("GhL", 9, 1, 1, 0, "L", 32, 32)
    hop("GlY", 10, 1, 3, 0, "Y")
    hop("GrY", 11, 1, 1, 0, "Y")
    got("TR", "TL")
    hop("ThR", 12, 0, 3, 0, "R", 0, 32)
    hop("ThL", 13, 0, 1, 0, "L", 32, 32)

    dk_sib.wait_recv()
    s2b[...] = (dkf[own_k, :] + drec[...].astype(F32)).astype(BF).reshape(CHIPS, T_ATT, LAT)

    def piece(i):
        return (
            pl.ds(pl.multiple_of(lax.div(i, 4) * 16, 16), 16),
            pl.ds(pl.multiple_of(lax.rem(i, 4) * 128, 128), 128),
        )

    rows_e, lanes_e = piece(e)
    own_piece = pltpu.make_async_copy(s2b.at[:, rows_e, lanes_e], ebuf.at[15], sem_l.at[10])
    own_piece.start()
    for i in range(1, N_EXP):
        te = lax.rem(e + i, N_EXP)
        rows_t, lanes_t = piece(te)
        remote(s2b.at[:, rows_t, lanes_t], ebuf.at[i - 1], sem_ds.at[8], sem_dr.at[8], c, te).start()

    for cp in w_in:
        cp.wait()
    for cp in rem:
        cp.wait_recv()

    swaps = {}

    def forward(dx):
        xt, xd = xg[0, dx], xg[1, dx]
        pbuf[dx, 0] = nn(xt, wg[...])
        pbuf[dx, 1] = nn(xt, wu[...])
        pbuf[dx, 2] = nt(xd, wd[...])
        swaps[dx] = remote(pbuf.at[dx], prec.at[dx], sem_ps.at[dx], sem_pr.at[dx], sib, e)
        swaps[dx].start()

    sends = {}

    def pass_on(kind, h, src, dst, to):
        index = 2 * kind + h
        cols = pl.ds(*COLS[h])
        sends[index] = remote(
            src.at[:, cols], dst.at[:, cols], sem_rs.at[index], sem_rr.at[index], to, e
        )
        sends[index].start()

    def passed(kind, h):
        sends[2 * kind + h].wait_recv()

    def backward(dx, done):
        swaps[dx].wait_recv()
        gate = pbuf[dx, 0] + prec[dx, 0]
        up = pbuf[dx, 1] + prec[dx, 1]
        act = pbuf[dx, 2] + prec[dx, 2]
        sig = 1.0 / (1.0 + jnp.exp(-gate))
        silu = gate * sig
        hid = (silu * up).astype(BF).astype(F32)
        parts[dx, :, pl.ds(0, EXTRA)] = split_score(jnp.sum(hid * act, axis=1, keepdims=True))
        ggb[...] = (act * up * sig * (1.0 + gate * (1.0 - sig))).astype(BF)
        ugb[...] = (act * silu).astype(BF)
        for h in range(2):

            def body(t, carry):
                at_col = h * (HALF // 2) + t * STEP
                cols = pl.ds(pl.multiple_of(at_col, STEP), STEP)
                val = nt(ggb[...], wg[cols, :]) + nt(ugb[...], wu[cols, :])
                parts[dx, :, pl.ds(pl.multiple_of(EXTRA + at_col, 128), STEP)] = val.astype(BF)
                return carry

            lax.fori_loop(0, HALF // 2 // STEP, body, 0)
            done(h)

    def merge(h, put, put_score, srcs):
        def summed(cols):
            val = srcs[0][:, cols].astype(F32)
            for ref in srcs[1:]:
                val = val + ref[:, cols].astype(F32)
            return val

        if h == 0:
            put_score(jnp.sum(summed(pl.ds(0, EXTRA)), axis=1, keepdims=True))

        def body(t, carry):
            cols = pl.ds(pl.multiple_of(EXTRA + h * (HALF // 2) + t * STEP, 128), STEP)
            put(cols, summed(cols).astype(BF))
            return carry

        lax.fori_loop(0, HALF // 2 // STEP, body, 0)

    def merge_into(h, dst, srcs):
        def put(cols, val):
            dst[:, cols] = val

        def put_score(score):
            dst[:, pl.ds(0, EXTRA)] = split_score(score)

        merge(h, put, put_score, srcs)

    mine, theirs = pl.ds(0, BLK), pl.ds(BLK, BLK)
    lo, hi = pl.ds(0, 32), pl.ds(32, 32)

    def to_right(h):
        pass_on(0, h, parts.at[1], rsx.at[0], right)

    def to_left(h):
        pass_on(1, h, parts.at[3], rsx.at[1], left)

    def to_mate(h):
        pass_on(2, h, parts.at[2, theirs], rsm, mate)

    got("GY")
    forward(0)
    got("GhR", "GhL")
    hop("Gh0Y", 14, 1, 2, 0, "Y", 0, 32)
    hop("Gh1Y", 15, 1, 2, 0, "Y", 32, 32)
    got("T1R", "T1L")
    hop("T1hR", 16, 0, 3, 1, "R", 0, 32)
    hop("T1hL", 17, 0, 1, 1, "L", 32, 32)
    got("GlY")
    forward(3)
    got("GrY")
    forward(1)
    backward(3, to_left)
    backward(1, to_right)
    backward(0, lambda h: None)

    own_piece.wait()
    take(ebuf.at[pl.ds(0, 15)], sem_dr.at[8])
    tot = ebuf[0].astype(F32)
    for i in range(1, N_EXP):
        tot = tot + ebuf[i].astype(F32)
    e8[...] = tot.astype(BF)
    for r in range(1, CHIPS):
        remote(e8.at[r], rbuf.at[CHIPS - 1 - r], sem_ds.at[1], sem_dr.at[1], chip_at(r), e).start()

    got("ThR", "ThL", "T1hR", "T1hL", "Gh0Y", "Gh1Y")
    forward(2)

    def to_mate_sum(h):
        passed(0, h)
        passed(1, h)
        merge_into(h, ysend, [parts.at[0, theirs], rsx.at[0, theirs], rsx.at[1, theirs]])
        pass_on(3, h, ysend, rsy, mate)

    to_mate_sum(0)
    backward(2, to_mate)
    for h in range(2):
        passed(2, h)
        merge_into(h, s2p, [parts.at[2, mine], rsm])
        pass_on(4, h, s2p.at[lo], rsf.at[0], right)
        pass_on(5, h, s2p.at[hi], rsf.at[1], left)
    to_mate_sum(1)
    for h in range(2):
        passed(4, h)
        pass_on(6, h, rsf.at[0], rs2.at[lo], right)
        passed(5, h)
        pass_on(7, h, rsf.at[1], rs2.at[hi], left)

    take(rbuf, sem_dr.at[1])
    tot = e8[0].astype(F32)
    for r in range(CHIPS - 1):
        tot = tot + rbuf[r].astype(F32)
    f1[...] = tot.astype(BF)
    own_final = pltpu.make_async_copy(f1, dlat.at[rows_e, lanes_e], sem_l.at[11])
    own_final.start()
    for i in range(1, N_EXP):
        te = lax.rem(e + i, N_EXP)
        remote(f1, dlat.at[rows_e, lanes_e], sem_ds.at[9], sem_dr.at[9], c, te).start()
    dq_ref[...] = dqs[...].reshape(T_ATT, 4, LAT)

    def put(cols, val):
        bsend[:, :, cols] = val.reshape(PAIRS, 2, STEP)

    def put_score(score):
        val = jnp.broadcast_to(score, (BLK, EXTRA)).astype(BF)
        bsend[:, :, pl.ds(0, EXTRA)] = val.reshape(PAIRS, 2, EXTRA)

    for h in range(2):
        passed(3, h)
        passed(6, h)
        passed(7, h)
        merge(h, put, put_score, [parts.at[0, mine], rsx.at[0, mine], rsx.at[1, mine], rsy, rs2])
        cols = pl.ds(*COLS[h])
        for i in range(N_EXP):
            te = lax.rem(e + i, N_EXP)
            for k in range(N_CORE):
                tc = lax.rem(core + k, 2)
                src = bsend.at[tc * N_EXP + te, :, cols]
                dst = back_ref.at[core * N_EXP + e, :, cols]
                if i == 0 and k == 0:
                    pltpu.make_async_copy(src, dst, sem_l.at[12 + h]).start()
                else:
                    remote(src, dst, sem_bs.at[h], sem_br.at[h], 2 * chip + tc, te).start()

    own_final.wait()
    take(ebuf.at[pl.ds(0, 15), 0], sem_dr.at[9])
    dlat_ref[...] = dlat[...]

    take(ra.at[0, pl.ds(0, 31)], sem_as.at[0])
    take(ra.at[1, pl.ds(0, 31)], sem_as.at[1])
    take(kbuf.at[pl.ds(0, 7 * T_ATT), :], sem_ks.at[0])
    lat_sib.wait_send()
    for cp in rem:
        cp.wait_send()
    for cp in hops.values():
        cp.wait_send()
    for cp in swaps.values():
        cp.wait_send()
    for cp in sends.values():
        cp.wait_send()
    dk_sib.wait_send()
    take(ebuf.at[pl.ds(0, 15)], sem_ds.at[8])
    take(rbuf, sem_ds.at[1])
    take(ebuf.at[pl.ds(0, 15), 0], sem_ds.at[9])
    for h in range(2):
        cols = pl.ds(*COLS[h])
        take(bsend.at[pl.ds(0, 31), :, cols], sem_bs.at[h])
        pltpu.make_async_copy(
            bsend.at[0, :, cols], back_ref.at[0, :, cols], sem_l.at[12 + h]
        ).wait()
        take(bsend.at[pl.ds(0, 31), :, cols], sem_br.at[h])


def fused(ids, prio, docs, tok, grd, wg, wu, wd, lat, q, do):
    vmem = pl.BlockSpec(memory_space=pltpu.VMEM)
    hbm = pl.BlockSpec(memory_space=pl.ANY)
    dma = pltpu.SemaphoreType.DMA

    def v(*shape, dtype=BF):
        return pltpu.VMEM(shape, dtype)

    return pl.pallas_call(
        kernel,
        out_shape=(
            jax.ShapeDtypeStruct((PAIRS, 2, OUTW), BF),
            jax.ShapeDtypeStruct((T_ATT, 4, LAT), BF),
            jax.ShapeDtypeStruct((T_ATT, LAT), BF),
        ),
        in_specs=[vmem] * 3 + [hbm] * 8,
        out_specs=(vmem, vmem, vmem),
        scratch_shapes=[
            v(2, 128, D),
            v(2, N_EXP, 2, D),
            v(2, PAIRS, 2, HALF),
            v(2, N_X, 2 * BLK, HALF),
            v(HALF, HID2),
            v(HALF, HID2),
            v(HID2, HALF),
            v(N_X, 3, 2 * BLK, HID2, dtype=F32),
            v(N_X, 3, 2 * BLK, HID2, dtype=F32),
            v(2 * BLK, HID2),
            v(2 * BLK, HID2),
            v(N_X, 2 * BLK, OUTW),
            v(2, 2 * BLK, OUTW),
            v(BLK, OUTW),
            v(BLK, OUTW),
            v(2, 32, OUTW),
            v(BLK, OUTW),
            v(BLK, OUTW),
            v(BLK, OUTW),
            v(PAIRS, 2, OUTW),
            v(T_ATT, 4, LAT),
            v(T_ATT, 4, LAT),
            v(ROWS_ATT, LAT),
            v(ROWS_ATT, LAT),
            v(ROWS_ATT, 128),
            v(ROWS_ATT, LAT),
            v(16 * T_ATT, KW),
            v(ROWS_ATT, 16 * T_ATT),
            v(ROWS_ATT, 16 * T_ATT),
            v(16 * T_ATT, LAT, dtype=F32),
            v(16 * T_ATT, LAT),
            v(CHIPS * T_ATT, LAT),
            v(CHIPS, T_ATT, LAT),
            v(16, CHIPS, 16, 128),
            v(CHIPS, 16, 128),
            v(CHIPS - 1, 16, 128),
            v(16, 128),
            v(T_ATT, LAT),
            dma((14,)),
            dma((2,)),
            dma((2,)),
            dma((2,)),
            dma((2,)),
            dma((3,)),
            dma((3,)),
            dma((18,)),
            dma((18,)),
            dma((4,)),
            dma((4,)),
            dma((16,)),
            dma((16,)),
            dma((2,)),
            dma((2,)),
            dma((10,)),
            dma((10,)),
        ],
        compiler_params=pltpu.CompilerParams(
            collective_id=0, has_side_effects=True, vmem_limit_bytes=58 * 1024 * 1024
        ),
        name="fused",
    )(ids, prio, docs, tok, grd, wg, wu, wd, lat, q, do)


def combine_kernel(ids_ref, prio_ref, gv_ref, back_ref, dq_in, dlat_in, dtok_ref, dg_ref, dq_ref, dlat_ref):
    ids = ids_ref[...]
    chosen, expert = route(ids, prio_ref[...])
    weight = jnp.zeros((PAIRS, 128), F32)
    for k in range(8):
        weight = weight + jnp.where(ids[k : k + 1, :] == expert, gv_ref[k : k + 1, :], 0.0)
    weight = weight * chosen
    w1 = weight.astype(BF)
    rest = weight - w1.astype(F32)
    w2 = rest.astype(BF)
    w3 = (rest - w2.astype(F32)).astype(BF)

    def body(t, carry):
        cols = pl.ds(pl.multiple_of(t * STEP, STEP), STEP)
        rows = back_ref[:, :, pl.ds(pl.multiple_of(EXTRA + t * STEP, 128), STEP)].reshape(PAIRS, STEP)
        dtok_ref[:, cols] = (tn(w3, rows) + tn(w2, rows) + tn(w1, rows)).astype(BF)
        return carry

    lax.fori_loop(0, HALF // STEP, body, 0)

    @pl.when(pl.program_id(0) == 0)
    def _():
        score = back_ref[:, :, pl.ds(0, EXTRA)].reshape(PAIRS, EXTRA).astype(F32)
        kept = chosen * score
        for k in range(8):
            own = jnp.where(ids[k : k + 1, :] == expert, kept, 0.0)
            dg_ref[k : k + 1, :] = jnp.sum(own, axis=0, keepdims=True).astype(BF)
        dq_ref[...] = dq_in[...]
        dlat_ref[...] = dlat_in[...]


def combine(ids, prio, gv, back, dq, dlat):
    def whole(shape):
        return pl.BlockSpec(shape, lambda h: (0,) * len(shape))

    return pl.pallas_call(
        combine_kernel,
        grid=(2,),
        out_shape=(
            jax.ShapeDtypeStruct((128, D), BF),
            jax.ShapeDtypeStruct((8, 128), BF),
            jax.ShapeDtypeStruct(dq.shape, BF),
            jax.ShapeDtypeStruct(dlat.shape, BF),
        ),
        in_specs=[
            whole((8, 128)),
            whole((1, 128)),
            whole((8, 128)),
            pl.BlockSpec((N_EXP, 2, OUTW), lambda h: (h, 0, 0)),
            whole(dq.shape),
            whole(dlat.shape),
        ],
        out_specs=(
            pl.BlockSpec((128, HALF), lambda h: (0, h)),
            whole((8, 128)),
            whole(dq.shape),
            whole(dlat.shape),
        ),
        name="combine",
    )(ids, prio, gv, back, dq, dlat)


def local(
    queries,
    latent,
    grad_out,
    doc_ids,
    tokens,
    token_grads,
    gate_values,
    expert_ids,
    gate_order,
    w_gate,
    w_up,
    w_down,
):
    ids = expert_ids.T
    back, dq, dlat = fused(
        ids,
        gate_order,
        doc_ids.reshape(1, T_ATT),
        tokens,
        token_grads,
        w_gate[0],
        w_up[0],
        w_down[0],
        latent,
        queries,
        grad_out,
    )
    d_tokens, d_gates, dq, dlat = combine(ids, gate_order, gate_values.T, back, dq, dlat)
    return (dq, dlat, d_tokens, d_gates.T)


def solution(mesh):
    in_specs = (
        P("ctx", "exp", None),
        P("ctx", None),
        P("ctx", "exp", None),
        P("ctx"),
        P(("ctx", "exp"), None),
        P(("ctx", "exp"), None),
        P(("ctx", "exp"), None),
        P(("ctx", "exp"), None),
        P(("ctx", "exp"), None),
        P("exp", None, "ctx"),
        P("exp", None, "ctx"),
        P("exp", "ctx", None),
    )
    out_specs = (
        P("ctx", "exp", None),
        P("ctx", None),
        P(("ctx", "exp"), None),
        P(("ctx", "exp"), None),
    )
    return jax.shard_map(local, mesh=mesh, in_specs=in_specs, out_specs=out_specs, check_vma=False)
```

time: 220 us -> 143 us (0.65)
  Pallas kernels: 190 us -> 142 us
  local copies, waits for them, and re-layouts: 18.9 us -> 0 us
  matrix products: 4.67 us -> 0 us
  other arithmetic: 4.39 us -> 0 us
    pallas_call x1 -> x2, Pallas kernels: 190 us -> 142 us  [the longest x1 133 us: fused(): pl.pallas_call(kernel, out_shape=(jax.ShapeDtypeStruct((PAIRS, 2, OUTW),...]
    reshape x3 -> x0, local copies, waits for them, and re-layouts: 5.15 us -> none  [the longest x1 1.72 us: local(): dq.reshape(queries.shape)]
    dot_general x5 -> x0, matrix products: 4.67 us -> none  [the longest x1 2.86 us: local(): jnp.einsum('tes,hesd->thd', weighting, rows[..., :HALF].astype(F32), prec...]
    unnamed x11 -> x0, local copies, waits for them, and re-layouts: 4.66 us -> none
    convert_element_type x1 -> x0, local copies, waits for them, and re-layouts: 3.78 us -> none  [local(): d_tokens.astype(BF)]
    dot_general x2 -> x0, local copies, waits for them, and re-layouts: 2.51 us -> none  [the longest x1 1.27 us: local(): jnp.einsum('tes,td->esd', picker, token_grads, preferred_element_type=F32)]
where the time goes in v2:
time: 143 us
  Pallas kernels  142 us (99%)
    pallas_call x1, Pallas kernels, fused(): pl.pallas_call(kernel, out_shape=(jax.ShapeDtypeStruct((PAIRS, 2, OUTW),...  133 us
    pallas_call x1, Pallas kernels, combine(): pl.pallas_call(combine_kernel, grid=(2,), out_shape=(jax.ShapeDtypeStruct...  9.29 us

profile of v2, /device:TPU:1, one launch (start us, length us, event | category | flops | bytes accessed | tf_op | source)
XLA Modules:
  0.0 142.9 jit_solution(14858906107223274653)
XLA Ops:
  0.6 133.0 %fused.1 = (bf16[32,2,3712]{2,1,0:T(2,128)(2,1)}, bf16[64,4,512]{2,1,0:T(4,128)(2,1)}, bf16[64,512]{1,0:T(8,128)(2,1)}) custom-call(s32[8,128]{1,0:T(8,128)} %bitcast.10, s32[1,128]{1,0:T(1,128)} %prio_ref.3, s32[1,64]{1,0:T(1,128)} %bitcast.13, bf16[128,7168]{1,0:T(8,128)(2,1)} %tok_hbm.1, bf16[128,7168]{1,0:T(8,128)(2,1)} %grd_hbm.1, ...), custom_call_target="tpu_custom_call" | custom-call | tf_op jit(solution)/shard_map/fused/pallas_call | solution.py:523
  133.6 9.3 %combine.1 = (bf16[128,7168]{1,0:T(8,128)(2,1)}, bf16[8,128]{1,0:T(8,128)(2,1)}, bf16[64,4,512]{2,1,0:T(4,128)(2,1)}, bf16[64,512]{1,0:T(8,128)(2,1)}) custom-call(s32[8,128]{1,0:T(8,128)} %bitcast.11, s32[1,128]{1,0:T(1,128)} %prio_ref.3, f32[8,128]{1,0:T(8,128)} %bitcast.12, bf16[32,2,3712]{2,1,0:T(2,128)(2,1)} %get-tuple-element.11.back_ref, ...), custom_call_target="tpu_custom_call" | custom-call | tf_op jit(solution)/shard_map/combine/pallas_call | solution.py:631

commit v3 on v2

--- a/solution.py
+++ b/solution.py
@@ -26,7 +26,9 @@
 EXTRA = 128
 OUTW = EXTRA + HALF
 STEP = 256
-COLS = ((0, EXTRA + HALF // 2), (EXTRA + HALF // 2, HALF // 2))
+HB = BLK // 2
+OFFSETS = (0, 1, -1, 2, -2, 3, -3, 4, -4, 5, -5, 6, -6, 7, -7, 8)
+COLS = (((0, OUTW),), ((0, EXTRA + HALF // 2), (EXTRA + HALF // 2, HALF // 2)))
 
 
 def nt(a, b):
@@ -149,17 +151,21 @@
 
         lax.fori_loop(0, D // 512, body, 0)
 
-    def scatter(arr):
-        for i in range(N_EXP):
-            te = lax.rem(e + i, N_EXP)
+    def scatter(arr, b):
+        for p in range(8):
+            te = lax.rem(e + (N_EXP - OFFSETS[8 * b + p]) % N_EXP, N_EXP)
             for k in range(N_CORE):
                 tc = lax.rem(core + k, 2)
                 src = snd.at[arr, te, :, pl.ds(pl.multiple_of(tc * HALF, HALF), HALF)]
-                dst = ra.at[arr, core * N_EXP + e]
-                if i == 0 and k == 0:
+                dst = ra.at[arr, b, core * 8 + p]
+                if b == 0 and p == 0 and k == 0:
                     pltpu.make_async_copy(src, dst, sem_l.at[8 + arr]).start()
                 else:
-                    remote(src, dst, sem_as.at[arr], sem_ar.at[arr], 2 * chip + tc, te).start()
+                    sem = 2 * b + arr
+                    remote(src, dst, sem_as.at[sem], sem_ar.at[sem], 2 * chip + tc, te).start()
+
+    def incoming(buf, b):
+        return buf.at[b, pl.ds(0, 15 + b)]
 
     pick(0)
     doc = lax.broadcasted_iota(jnp.int32, (128, T_ATT), 0)
@@ -179,9 +185,11 @@
         row = core * 512 + (CHIPS - r) * T_ATT
         dst = kbuf.at[pl.ds(pl.multiple_of(row, T_ATT), T_ATT), :]
         remote(kbuf.at[own_b, :], dst, sem_ks.at[0], sem_kr.at[0], chip_at(r), e).start()
-    scatter(0)
+    scatter(0, 0)
     pick(1)
-    scatter(1)
+    scatter(1, 0)
+    scatter(0, 1)
+    scatter(1, 1)
     rem = [
         remote(wg_hbm.at[oth_d, :], wg.at[:, pl.ds(lane0, SHARD)], sem_ws.at[0], sem_wr.at[0], sib, e),
         remote(wu_hbm.at[oth_d, :], wu.at[:, pl.ds(lane0, SHARD)], sem_ws.at[1], sem_wr.at[1], sib, e),
@@ -198,50 +206,80 @@
     col_q = lax.broadcasted_iota(jnp.int32, (ROWS_ATT, T_ATT), 1)
     qd[...] = nn(jnp.where(row_q == col_q, 1.0, 0.0).astype(BF), onehot).astype(BF)
 
-    take(kbuf.at[pl.ds(0, 7 * T_ATT), :], sem_kr.at[0])
-    lat_sib = remote(kbuf.at[own_k, :], kbuf.at[own_k, :], sem_ks.at[1], sem_kr.at[1], sib, e)
-    lat_sib.start()
-
     hops = {}
-
-    def hop(name, index, arr, dx, dy, way, lo=0, n=BLK):
+    names = {}
+
+    def hop(b, name, arr, dx, dy, way, lo=0, n=HB):
         if way == "R":
             to, tx, ty = right, (dx + 3) % 4, dy
         elif way == "L":
             to, tx, ty = left, (dx + 1) % 4, dy
         else:
             to, tx, ty = mate, dx, 1 - dy
-        hops[name] = remote(
-            xg.at[arr, dx, pl.ds(dy * BLK + lo, n), :],
-            xg.at[arr, tx, pl.ds(ty * BLK + lo, n), :],
+        index = 18 * b + names.setdefault(name, len(names))
+        hops[b, name] = remote(
+            xg.at[arr, b, dx, pl.ds(dy * HB + lo, n), :],
+            xg.at[arr, b, tx, pl.ds(ty * HB + lo, n), :],
             sem_gs.at[index],
             sem_gr.at[index],
             to,
             e,
         )
-        hops[name].start()
-
-    def got(*names):
-        for name in names:
-            hops[name].wait_recv()
-
-    def repack(arr):
-        pltpu.make_async_copy(
-            snd.at[0, 0, :, pl.ds(0, HALF)], ra.at[arr, 0], sem_l.at[8 + arr]
-        ).wait()
-        take(ra.at[arr, pl.ds(0, 31)], sem_ar.at[arr])
+        hops[b, name].start()
+
+    def got(b, *which):
+        for name in which:
+            hops[b, name].wait_recv()
+
+    def repack(arr, b):
+        if b == 0:
+            pltpu.make_async_copy(
+                snd.at[0, 0, :, pl.ds(0, HALF)], ra.at[arr, 0, 0], sem_l.at[8 + arr]
+            ).wait()
+        take(incoming(ra.at[arr], b), sem_ar.at[2 * b + arr])
 
         def body(t, carry):
             cols = pl.ds(pl.multiple_of(t * 512, 512), 512)
-            xg[arr, 0, pl.ds(0, BLK), cols] = ra[arr, :, :, cols].reshape(BLK, 512)
+            xg[arr, b, 0, pl.ds(0, HB), cols] = ra[arr, b, :, :, cols].reshape(HB, 512)
             return carry
 
         lax.fori_loop(0, HALF // 512, body, 0)
 
-    repack(0)
-    hop("TY", 0, 0, 0, 0, "Y")
-    hop("TR", 1, 0, 0, 0, "R")
-    hop("TL", 2, 0, 0, 0, "L")
+    def hops_own(b):
+        repack(0, b)
+        hop(b, "TY", 0, 0, 0, "Y")
+        hop(b, "TR", 0, 0, 0, "R")
+        hop(b, "TL", 0, 0, 0, "L")
+        repack(1, b)
+        hop(b, "GR", 1, 0, 0, "R")
+        hop(b, "GL", 1, 0, 0, "L")
+        hop(b, "GY", 1, 0, 0, "Y")
+
+    def hops_second(b):
+        got(b, "TY")
+        hop(b, "T1R", 0, 0, 1, "R")
+        hop(b, "T1L", 0, 0, 1, "L")
+        got(b, "GR", "GL")
+        hop(b, "GlY", 1, 3, 0, "Y")
+        hop(b, "GrY", 1, 1, 0, "Y")
+        hop(b, "GhR", 1, 3, 0, "R", 0, HB // 2)
+        hop(b, "GhL", 1, 1, 0, "L", HB // 2, HB // 2)
+        got(b, "TR", "TL")
+        hop(b, "ThR", 0, 3, 0, "R", 0, HB // 2)
+        hop(b, "ThL", 0, 1, 0, "L", HB // 2, HB // 2)
+
+    def hops_third(b):
+        got(b, "GhR", "GhL")
+        hop(b, "Gh0Y", 1, 2, 0, "Y", 0, HB // 2)
+        hop(b, "Gh1Y", 1, 2, 0, "Y", HB // 2, HB // 2)
+        got(b, "T1R", "T1L")
+        hop(b, "T1hR", 0, 3, 1, "R", 0, HB // 2)
+        hop(b, "T1hL", 0, 1, 1, "L", HB // 2, HB // 2)
+
+    hops_own(0)
+    take(kbuf.at[pl.ds(0, 7 * T_ATT), :], sem_kr.at[0])
+    lat_sib = remote(kbuf.at[own_k, :], kbuf.at[own_k, :], sem_ks.at[1], sem_kr.at[1], sib, e)
+    lat_sib.start()
 
     lat_sib.wait_recv()
 
@@ -265,13 +303,7 @@
 
     lax.fori_loop(0, ROWS_ATT // 64, att, 0)
 
-    repack(1)
-    hop("GR", 3, 1, 0, 0, "R")
-    hop("GL", 4, 1, 0, 0, "L")
-    hop("GY", 5, 1, 0, 0, "Y")
-    got("TY")
-    hop("T1R", 6, 0, 0, 1, "R")
-    hop("T1L", 7, 0, 0, 1, "L")
+    hops_second(0)
 
     def dkeys(k, carry):
         rows = pl.ds(pl.multiple_of(k * 128, 128), 128)
@@ -284,14 +316,162 @@
     dk_sib = remote(dkb.at[oth_k, :], drec, sem_ds.at[0], sem_dr.at[0], sib, e)
     dk_sib.start()
 
-    got("GR", "GL")
-    hop("GhR", 8, 1, 3, 0, "R", 0, 32)
-    hop("GhL", 9, 1, 1, 0, "L", 32, 32)
-    hop("GlY", 10, 1, 3, 0, "Y")
-    hop("GrY", 11, 1, 1, 0, "Y")
-    got("TR", "TL")
-    hop("ThR", 12, 0, 3, 0, "R", 0, 32)
-    hop("ThL", 13, 0, 1, 0, "L", 32, 32)
+    for cp in w_in:
+        cp.wait()
+    for cp in rem:
+        cp.wait_recv()
+
+    swaps = {}
+
+    def forward(b, dx):
+        xt, xd = xg[0, b, dx], xg[1, b, dx]
+        pbuf[b, dx, 0] = nn(xt, wg[...])
+        pbuf[b, dx, 1] = nn(xt, wu[...])
+        pbuf[b, dx, 2] = nt(xd, wd[...])
+        index = 4 * b + dx
+        swaps[b, dx] = remote(
+            pbuf.at[b, dx], prec.at[b, dx], sem_ps.at[index], sem_pr.at[index], sib, e
+        )
+        swaps[b, dx].start()
+
+    sends = {}
+
+    def pass_on(kind, b, h, src, dst, to):
+        index = 3 * kind + b + h
+        cols = pl.ds(*COLS[b][h])
+        sends[kind, b, h] = remote(
+            src.at[:, cols], dst.at[:, cols], sem_rs.at[index], sem_rr.at[index], to, e
+        )
+        sends[kind, b, h].start()
+
+    def passed(kind, b, h):
+        sends[kind, b, h].wait_recv()
+
+    def wide(b, h):
+        start, n = COLS[b][h]
+        first = max(start - EXTRA, 0)
+        return first, (start + n - EXTRA - first) // STEP
+
+    def backward(b, dx, done):
+        swaps[b, dx].wait_recv()
+        gate = pbuf[b, dx, 0] + prec[b, dx, 0]
+        up = pbuf[b, dx, 1] + prec[b, dx, 1]
+        act = pbuf[b, dx, 2] + prec[b, dx, 2]
+        sig = 1.0 / (1.0 + jnp.exp(-gate))
+        silu = gate * sig
+        hid = (silu * up).astype(BF).astype(F32)
+        parts[b, dx, :, pl.ds(0, EXTRA)] = split_score(jnp.sum(hid * act, axis=1, keepdims=True))
+        ggb[...] = (act * up * sig * (1.0 + gate * (1.0 - sig))).astype(BF)
+        ugb[...] = (act * silu).astype(BF)
+        for h in range(len(COLS[b])):
+            first, steps = wide(b, h)
+
+            def body(t, carry):
+                at_col = first + t * STEP
+                cols = pl.ds(pl.multiple_of(at_col, STEP), STEP)
+                val = nt(ggb[...], wg[cols, :]) + nt(ugb[...], wu[cols, :])
+                parts[b, dx, :, pl.ds(pl.multiple_of(EXTRA + at_col, 128), STEP)] = val.astype(BF)
+                return carry
+
+            lax.fori_loop(0, steps, body, 0)
+            if done is not None:
+                done(b, h)
+
+    def merge(b, h, put, put_score, srcs):
+        def summed(cols):
+            val = srcs[0][:, cols].astype(F32)
+            for ref in srcs[1:]:
+                val = val + ref[:, cols].astype(F32)
+            return val
+
+        if h == 0:
+            put_score(jnp.sum(summed(pl.ds(0, EXTRA)), axis=1, keepdims=True))
+        first, steps = wide(b, h)
+
+        def body(t, carry):
+            cols = pl.ds(pl.multiple_of(EXTRA + first + t * STEP, 128), STEP)
+            put(cols, summed(cols).astype(BF))
+            return carry
+
+        lax.fori_loop(0, steps, body, 0)
+
+    def merge_into(b, h, dst, srcs):
+        def put(cols, val):
+            dst[:, cols] = val
+
+        def put_score(score):
+            dst[:, pl.ds(0, EXTRA)] = split_score(score)
+
+        merge(b, h, put, put_score, srcs)
+
+    mine, theirs = pl.ds(0, HB), pl.ds(HB, HB)
+    lo, hi = pl.ds(0, HB // 2), pl.ds(HB // 2, HB // 2)
+
+    def to_right(b, h):
+        pass_on(0, b, h, parts.at[b, 1], rsx.at[b, 0], right)
+
+    def to_left(b, h):
+        pass_on(1, b, h, parts.at[b, 3], rsx.at[b, 1], left)
+
+    def to_mate(b, h):
+        pass_on(2, b, h, parts.at[b, 2, theirs], rsm.at[b], mate)
+
+    def to_mate_sum(b, h):
+        passed(0, b, h)
+        passed(1, b, h)
+        merge_into(
+            b, h, ysend.at[b], [parts.at[b, 0, theirs], rsx.at[b, 0, theirs], rsx.at[b, 1, theirs]]
+        )
+        pass_on(3, b, h, ysend.at[b], rsy.at[b], mate)
+
+    def to_far(b, h):
+        passed(2, b, h)
+        merge_into(b, h, s2p.at[b], [parts.at[b, 2, mine], rsm.at[b]])
+        pass_on(4, b, h, s2p.at[b, lo], rsf.at[b, 0], right)
+        pass_on(5, b, h, s2p.at[b, hi], rsf.at[b, 1], left)
+
+    def to_far_again(b, h):
+        passed(4, b, h)
+        pass_on(6, b, h, rsf.at[b, 0], rs2.at[b, lo], right)
+        passed(5, b, h)
+        pass_on(7, b, h, rsf.at[b, 1], rs2.at[b, hi], left)
+
+    def give_back(b, h):
+        def put(cols, val):
+            bsend[b, :, :, cols] = val.reshape(16, 2, STEP)
+
+        def put_score(score):
+            val = jnp.broadcast_to(score, (HB, EXTRA)).astype(BF)
+            bsend[b, :, :, pl.ds(0, EXTRA)] = val.reshape(16, 2, EXTRA)
+
+        passed(3, b, h)
+        passed(6, b, h)
+        passed(7, b, h)
+        merge(
+            b,
+            h,
+            put,
+            put_score,
+            [parts.at[b, 0, mine], rsx.at[b, 0, mine], rsx.at[b, 1, mine], rsy.at[b], rs2.at[b]],
+        )
+        cols = pl.ds(*COLS[b][h])
+        for p in range(8):
+            te = lax.rem(e + OFFSETS[8 * b + p] % N_EXP, N_EXP)
+            for k in range(N_CORE):
+                tc = lax.rem(core + k, 2)
+                src = bsend.at[b, tc * 8 + p, :, cols]
+                dst = back_ref.at[core * N_EXP + e, :, cols]
+                if b == 0 and p == 0 and k == 0:
+                    pltpu.make_async_copy(src, dst, sem_l.at[12]).start()
+                else:
+                    remote(
+                        src, dst, sem_bs.at[b + h], sem_br.at[b + h], 2 * chip + tc, te
+                    ).start()
+
+    got(0, "GY")
+    forward(0, 0)
+    hops_own(1)
+    hops_third(0)
 
     dk_sib.wait_recv()
     s2b[...] = (dkf[own_k, :] + drec[...].astype(F32)).astype(BF).reshape(CHIPS, T_ATT, LAT)
@@ -310,110 +490,29 @@
         rows_t, lanes_t = piece(te)
         remote(s2b.at[:, rows_t, lanes_t], ebuf.at[i - 1], sem_ds.at[8], sem_dr.at[8], c, te).start()
 
-    for cp in w_in:
-        cp.wait()
-    for cp in rem:
-        cp.wait_recv()
-
-    swaps = {}
-
-    def forward(dx):
-        xt, xd = xg[0, dx], xg[1, dx]
-        pbuf[dx, 0] = nn(xt, wg[...])
-        pbuf[dx, 1] = nn(xt, wu[...])
-        pbuf[dx, 2] = nt(xd, wd[...])
-        swaps[dx] = remote(pbuf.at[dx], prec.at[dx], sem_ps.at[dx], sem_pr.at[dx], sib, e)
-        swaps[dx].start()
-
-    sends = {}
-
-    def pass_on(kind, h, src, dst, to):
-        index = 2 * kind + h
-        cols = pl.ds(*COLS[h])
-        sends[index] = remote(
-            src.at[:, cols], dst.at[:, cols], sem_rs.at[index], sem_rr.at[index], to, e
-        )
-        sends[index].start()
-
-    def passed(kind, h):
-        sends[2 * kind + h].wait_recv()
-
-    def backward(dx, done):
-        swaps[dx].wait_recv()
-        gate = pbuf[dx, 0] + prec[dx, 0]
-        up = pbuf[dx, 1] + prec[dx, 1]
-        act = pbuf[dx, 2] + prec[dx, 2]
-        sig = 1.0 / (1.0 + jnp.exp(-gate))
-        silu = gate * sig
-        hid = (silu * up).astype(BF).astype(F32)
-        parts[dx, :, pl.ds(0, EXTRA)] = split_score(jnp.sum(hid * act, axis=1, keepdims=True))
-        ggb[...] = (act * up * sig * (1.0 + gate * (1.0 - sig))).astype(BF)
-        ugb[...] = (act * silu).astype(BF)
-        for h in range(2):
-
-            def body(t, carry):
-                at_col = h * (HALF // 2) + t * STEP
-                cols = pl.ds(pl.multiple_of(at_col, STEP), STEP)
-                val = nt(ggb[...], wg[cols, :]) + nt(ugb[...], wu[cols, :])
-                parts[dx, :, pl.ds(pl.multiple_of(EXTRA + at_col, 128), STEP)] = val.astype(BF)
-                return carry
-
-            lax.fori_loop(0, HALF // 2 // STEP, body, 0)
-            done(h)
-
-    def merge(h, put, put_score, srcs):
-        def summed(cols):
-            val = srcs[0][:, cols].astype(F32)
-            for ref in srcs[1:]:
-                val = val + ref[:, cols].astype(F32)
-            return val
-
-        if h == 0:
-            put_score(jnp.sum(summed(pl.ds(0, EXTRA)), axis=1, keepdims=True))
-
-        def body(t, carry):
-            cols = pl.ds(pl.multiple_of(EXTRA + h * (HALF // 2) + t * STEP, 128), STEP)
-            put(cols, summed(cols).astype(BF))
-            return carry
-
-        lax.fori_loop(0, HALF // 2 // STEP, body, 0)
-
-    def merge_into(h, dst, srcs):
-        def put(cols, val):
-            dst[:, cols] = val
-
-        def put_score(score):
-            dst[:, pl.ds(0, EXTRA)] = split_score(score)
-
-        merge(h, put, put_score, srcs)
-
-    mine, theirs = pl.ds(0, BLK), pl.ds(BLK, BLK)
-    lo, hi = pl.ds(0, 32), pl.ds(32, 32)
-
-    def to_right(h):
-        pass_on(0, h, parts.at[1], rsx.at[0], right)
-
-    def to_left(h):
-        pass_on(1, h, parts.at[3], rsx.at[1], left)
-
-    def to_mate(h):
-        pass_on(2, h, parts.at[2, theirs], rsm, mate)
-
-    got("GY")
-    forward(0)
-    got("GhR", "GhL")
-    hop("Gh0Y", 14, 1, 2, 0, "Y", 0, 32)
-    hop("Gh1Y", 15, 1, 2, 0, "Y", 32, 32)
-    got("T1R", "T1L")
-    hop("T1hR", 16, 0, 3, 1, "R", 0, 32)
-    hop("T1hL", 17, 0, 1, 1, "L", 32, 32)
-    got("GlY")
-    forward(3)
-    got("GrY")
-    forward(1)
-    backward(3, to_left)
-    backward(1, to_right)
-    backward(0, lambda h: None)
+    got(0, "GlY")
+    forward(0, 3)
+    got(0, "GrY")
+    forward(0, 1)
+    backward(0, 3, to_left)
+    backward(0, 1, to_right)
+    hops_second(1)
+    got(0, "ThR", "ThL", "T1hR", "T1hL", "Gh0Y", "Gh1Y")
+    forward(0, 2)
+    backward(0, 0, None)
+    backward(0, 2, to_mate)
+    got(1, "GY")
+    forward(1, 0)
+    hops_third(1)
+    to_mate_sum(0, 0)
+    to_far(0, 0)
+    got(1, "GlY")
+    forward(1, 3)
+    got(1, "GrY")
+    forward(1, 1)
+    backward(1, 3, to_left)
+    backward(1, 1, to_right)
+    to_far_again(0, 0)
 
     own_piece.wait()
     take(ebuf.at[pl.ds(0, 15)], sem_dr.at[8])
@@ -423,29 +522,18 @@
     e8[...] = tot.astype(BF)
     for r in range(1, CHIPS):
         remote(e8.at[r], rbuf.at[CHIPS - 1 - r], sem_ds.at[1], sem_dr.at[1], chip_at(r), e).start()
-
-    got("ThR", "ThL", "T1hR", "T1hL", "Gh0Y", "Gh1Y")
-    forward(2)
-
-    def to_mate_sum(h):
-        passed(0, h)
-        passed(1, h)
-        merge_into(h, ysend, [parts.at[0, theirs], rsx.at[0, theirs], rsx.at[1, theirs]])
-        pass_on(3, h, ysend, rsy, mate)
-
-    to_mate_sum(0)
-    backward(2, to_mate)
-    for h in range(2):
-        passed(2, h)
-        merge_into(h, s2p, [parts.at[2, mine], rsm])
-        pass_on(4, h, s2p.at[lo], rsf.at[0], right)
-        pass_on(5, h, s2p.at[hi], rsf.at[1], left)
-    to_mate_sum(1)
-    for h in range(2):
-        passed(4, h)
-        pass_on(6, h, rsf.at[0], rs2.at[lo], right)
-        passed(5, h)
-        pass_on(7, h, rsf.at[1], rs2.at[hi], left)
+    backward(1, 0, None)
+
+    got(1, "ThR", "ThL", "T1hR", "T1hL", "Gh0Y", "Gh1Y")
+    forward(1, 2)
+    to_mate_sum(1, 0)
+    backward(1, 2, to_mate)
+    give_back(0, 0)
+    to_far(1, 0)
+    to_far(1, 1)
+    to_mate_sum(1, 1)
+    to_far_again(1, 0)
+    to_far_again(1, 1)
 
     take(rbuf, sem_dr.at[1])
     tot = e8[0].astype(F32)
@@ -459,36 +547,16 @@
         remote(f1, dlat.at[rows_e, lanes_e], sem_ds.at[9], sem_dr.at[9], c, te).start()
     dq_ref[...] = dqs[...].reshape(T_ATT, 4, LAT)
 
-    def put(cols, val):
-        bsend[:, :, cols] = val.reshape(PAIRS, 2, STEP)
-
-    def put_score(score):
-        val = jnp.broadcast_to(score, (BLK, EXTRA)).astype(BF)
-        bsend[:, :, pl.ds(0, EXTRA)] = val.reshape(PAIRS, 2, EXTRA)
-
-    for h in range(2):
-        passed(3, h)
-        passed(6, h)
-        passed(7, h)
-        merge(h, put, put_score, [parts.at[0, mine], rsx.at[0, mine], rsx.at[1, mine], rsy, rs2])
-        cols = pl.ds(*COLS[h])
-        for i in range(N_EXP):
-            te = lax.rem(e + i, N_EXP)
-            for k in range(N_CORE):
-                tc = lax.rem(core + k, 2)
-                src = bsend.at[tc * N_EXP + te, :, cols]
-                dst = back_ref.at[core * N_EXP + e, :, cols]
-                if i == 0 and k == 0:
-                    pltpu.make_async_copy(src, dst, sem_l.at[12 + h]).start()
-                else:
-                    remote(src, dst, sem_bs.at[h], sem_br.at[h], 2 * chip + tc, te).start()
+    give_back(1, 0)
+    give_back(1, 1)
 
     own_final.wait()
     take(ebuf.at[pl.ds(0, 15), 0], sem_dr.at[9])
     dlat_ref[...] = dlat[...]
 
-    take(ra.at[0, pl.ds(0, 31)], sem_as.at[0])
-    take(ra.at[1, pl.ds(0, 31)], sem_as.at[1])
+    for b in range(2):
+        for arr in range(2):
+            take(incoming(ra.at[arr], b), sem_as.at[2 * b + arr])
     take(kbuf.at[pl.ds(0, 7 * T_ATT), :], sem_ks.at[0])
     lat_sib.wait_send()
     for cp in rem:
@@ -503,13 +571,11 @@
     take(ebuf.at[pl.ds(0, 15)], sem_ds.at[8])
     take(rbuf, sem_ds.at[1])
     take(ebuf.at[pl.ds(0, 15), 0], sem_ds.at[9])
-    for h in range(2):
-        cols = pl.ds(*COLS[h])
-        take(bsend.at[pl.ds(0, 31), :, cols], sem_bs.at[h])
-        pltpu.make_async_copy(
-            bsend.at[0, :, cols], back_ref.at[0, :, cols], sem_l.at[12 + h]
-        ).wait()
-        take(bsend.at[pl.ds(0, 31), :, cols], sem_br.at[h])
+    pltpu.make_async_copy(bsend.at[0, 0], back_ref.at[0], sem_l.at[12]).wait()
+    for sems in (sem_bs, sem_br):
+        take(incoming(bsend, 0), sems.at[0])
+        for h in range(2):
+            take(bsend.at[1, :, :, pl.ds(*COLS[1][h])], sems.at[1 + h])
 
 
 def fused(ids, prio, docs, tok, grd, wg, wu, wd, lat, q, do):
@@ -532,24 +598,24 @@
         scratch_shapes=[
             v(2, 128, D),
             v(2, N_EXP, 2, D),
-            v(2, PAIRS, 2, HALF),
-            v(2, N_X, 2 * BLK, HALF),
+            v(2, 2, 16, 2, HALF),
+            v(2, 2, N_X, 2 * HB, HALF),
             v(HALF, HID2),
             v(HALF, HID2),
             v(HID2, HALF),
-            v(N_X, 3, 2 * BLK, HID2, dtype=F32),
-            v(N_X, 3, 2 * BLK, HID2, dtype=F32),
-            v(2 * BLK, HID2),
-            v(2 * BLK, HID2),
-            v(N_X, 2 * BLK, OUTW),
-            v(2, 2 * BLK, OUTW),
-            v(BLK, OUTW),
-            v(BLK, OUTW),
-            v(2, 32, OUTW),
-            v(BLK, OUTW),
-            v(BLK, OUTW),
-            v(BLK, OUTW),
-            v(PAIRS, 2, OUTW),
+            v(2, N_X, 3, 2 * HB, HID2, dtype=F32),
+            v(2, N_X, 3, 2 * HB, HID2, dtype=F32),
+            v(2 * HB, HID2),
+            v(2 * HB, HID2),
+            v(2, N_X, 2 * HB, OUTW),
+            v(2, 2, 2 * HB, OUTW),
+            v(2, HB, OUTW),
+            v(2, HB, OUTW),
+            v(2, 2, HB // 2, OUTW),
+            v(2, HB, OUTW),
+            v(2, HB, OUTW),
+            v(2, HB, OUTW),
+            v(2, 16, 2, OUTW),
             v(T_ATT, 4, LAT),
             v(T_ATT, 4, LAT),
             v(ROWS_ATT, LAT),
@@ -568,21 +634,21 @@
             v(CHIPS - 1, 16, 128),
             v(16, 128),
             v(T_ATT, LAT),
-            dma((14,)),
-            dma((2,)),
-            dma((2,)),
+            dma((13,)),
+            dma((4,)),
+            dma((4,)),
             dma((2,)),
             dma((2,)),
             dma((3,)),
             dma((3,)),
-            dma((18,)),
-            dma((18,)),
-            dma((4,)),
-            dma((4,)),
-            dma((16,)),
-            dma((16,)),
-            dma((2,)),
-            dma((2,)),
+            dma((36,)),
+            dma((36,)),
+            dma((8,)),
+            dma((8,)),
+            dma((24,)),
+            dma((24,)),
+            dma((3,)),
+            dma((3,)),
             dma((10,)),
             dma((10,)),
         ],
@@ -600,18 +666,14 @@
     for k in range(8):
         weight = weight + jnp.where(ids[k : k + 1, :] == expert, gv_ref[k : k + 1, :], 0.0)
     weight = weight * chosen
-    w1 = weight.astype(BF)
-    rest = weight - w1.astype(F32)
-    w2 = rest.astype(BF)
-    w3 = (rest - w2.astype(F32)).astype(BF)
-
-    def body(t, carry):
-        cols = pl.ds(pl.multiple_of(t * STEP, STEP), STEP)
-        rows = back_ref[:, :, pl.ds(pl.multiple_of(EXTRA + t * STEP, 128), STEP)].reshape(PAIRS, STEP)
-        dtok_ref[:, cols] = (tn(w3, rows) + tn(w2, rows) + tn(w1, rows)).astype(BF)
-        return carry
-
-    lax.fori_loop(0, HALF // STEP, body, 0)
+    w1 = weight.astype(BF).astype(F32)
+    w2 = (weight - w1).astype(BF).astype(F32)
+    w3 = weight - w1 - w2
+    terms = jnp.concatenate([w3, w2, w1, jnp.zeros((PAIRS, 128), F32)], axis=0).T.astype(BF)
+    for t in range(HALF // 512):
+        rows = back_ref[:, :, pl.ds(EXTRA + t * 512, 512)].reshape(PAIRS, 512)
+        stacked = jnp.concatenate([rows, rows, rows, rows], axis=0)
+        dtok_ref[:, pl.ds(t * 512, 512)] = nn(terms, stacked).astype(BF)
 
     @pl.when(pl.program_id(0) == 0)
     def _():

time: 143 us -> 139 us (0.972)
  Pallas kernels: 142 us -> 138 us
    pallas_call x1, Pallas kernels: 9.29 us -> 3.58 us  [combine(): pl.pallas_call(combine_kernel, grid=(2,), out_shape=(jax.ShapeDtypeStruct...]
where the time goes in v3:
time: 139 us; the launch traced here: 138 us
  Pallas kernels  138 us (99%)
    pallas_call x1, Pallas kernels, fused(): pl.pallas_call(kernel, out_shape=(jax.ShapeDtypeStruct((PAIRS, 2, OUTW),...  134 us
    pallas_call x1, Pallas kernels, combine(): pl.pallas_call(combine_kernel, grid=(2,), out_shape=(jax.ShapeDtypeStruct...  3.58 us

profile of v3, /device:TPU:1, one launch (start us, length us, event | category | flops | bytes accessed | tf_op | source)
XLA Modules:
  0.0 138.4 jit_solution(13094430131142032171)
XLA Ops:
  0.6 134.2 %fused.1 = (bf16[32,2,3712]{2,1,0:T(2,128)(2,1)}, bf16[64,4,512]{2,1,0:T(4,128)(2,1)}, bf16[64,512]{1,0:T(8,128)(2,1)}) custom-call(s32[8,128]{1,0:T(8,128)} %bitcast.10, s32[1,128]{1,0:T(1,128)} %prio_ref.3, s32[1,64]{1,0:T(1,128)} %bitcast.13, bf16[128,7168]{1,0:T(8,128)(2,1)} %tok_hbm.1, bf16[128,7168]{1,0:T(8,128)(2,1)} %grd_hbm.1, ...), custom_call_target="tpu_custom_call" | custom-call | tf_op jit(solution)/shard_map/fused/pallas_call | solution.py:589
  134.9 3.6 %combine.1 = (bf16[128,7168]{1,0:T(8,128)(2,1)}, bf16[8,128]{1,0:T(8,128)(2,1)}, bf16[64,4,512]{2,1,0:T(4,128)(2,1)}, bf16[64,512]{1,0:T(8,128)(2,1)}) custom-call(s32[8,128]{1,0:T(8,128)} %bitcast.11, s32[1,128]{1,0:T(1,128)} %prio_ref.3, f32[8,128]{1,0:T(8,128)} %bitcast.12, bf16[32,2,3712]{2,1,0:T(2,128)(2,1)} %get-tuple-element.11.back_ref, ...), custom_call_target="tpu_custom_call" | custom-call | tf_op jit(solution)/shard_map/combine/pallas_call | solution.py:693

commit v4 on v3

--- a/solution.py
+++ b/solution.py
@@ -67,7 +67,7 @@
     ids_ref, prio_ref, docs_ref, tok_hbm, grd_hbm, wg_hbm, wu_hbm, wd_hbm, lat_hbm, q_hbm, do_hbm,
     back_ref, dq_ref, dlat_ref,
     rows_v, snd, ra, xg, wg, wu, wd, pbuf, prec, ggb, ugb, parts, rsx, rsm, s2p, rsf, rs2, ysend, rsy, bsend,
-    q3, do3, qs, dos, qd, dqs, kbuf, dsb, pwb, dkf, dkb, drec, s2b, ebuf, e8, rbuf, f1, dlat,
+    q3, do3, qs, dos, qd, dqs, kbuf, dsb, pwb, dkf, dkb, drec, s2b, ebuf, e8, rbuf, f1, gbuf,
     sem_l, sem_as, sem_ar, sem_ks, sem_kr, sem_ws, sem_wr, sem_gs, sem_gr, sem_ps, sem_pr,
     sem_rs, sem_rr, sem_bs, sem_br, sem_ds, sem_dr,
 ):
@@ -98,6 +98,11 @@
 
     def take(ref, sem):
         pltpu.make_async_copy(ref, ref, sem).wait()
+
+    def entry(off, k):
+        tc = lax.rem(core + k, 2)
+        base = mate - core if off % 2 else 2 * chip
+        return base + tc, tc
 
     def chip_at(r):
         return 2 * lax.rem(chip + r, CHIPS) + core
@@ -131,9 +136,11 @@
     for r in range(1, CHIPS):
         pl.semaphore_signal(bar, inc=1, device_id=at(chip_at(r), e), device_id_type=MESH)
     for i in range(1, N_EXP):
+        te = lax.rem(e + i, N_EXP)
         for k in range(N_CORE):
-            to = at(2 * chip + lax.rem(core + k, 2), lax.rem(e + i, N_EXP))
-            pl.semaphore_signal(bar, inc=1, device_id=to, device_id_type=MESH)
+            pl.semaphore_signal(bar, inc=1, device_id=at(entry(i, k)[0], te), device_id_type=MESH)
+        if i % 2:
+            pl.semaphore_signal(bar, inc=1, device_id=at(c, te), device_id_type=MESH)
     for cp in att_in + w_in:
         cp.start()
 
@@ -155,14 +162,14 @@
         for p in range(8):
             te = lax.rem(e + (N_EXP - OFFSETS[8 * b + p]) % N_EXP, N_EXP)
             for k in range(N_CORE):
-                tc = lax.rem(core + k, 2)
+                to, tc = entry(OFFSETS[8 * b + p], k)
                 src = snd.at[arr, te, :, pl.ds(pl.multiple_of(tc * HALF, HALF), HALF)]
                 dst = ra.at[arr, b, core * 8 + p]
                 if b == 0 and p == 0 and k == 0:
                     pltpu.make_async_copy(src, dst, sem_l.at[8 + arr]).start()
                 else:
                     sem = 2 * b + arr
-                    remote(src, dst, sem_as.at[sem], sem_ar.at[sem], 2 * chip + tc, te).start()
+                    remote(src, dst, sem_as.at[sem], sem_ar.at[sem], to, te).start()
 
     def incoming(buf, b):
         return buf.at[b, pl.ds(0, 15 + b)]
@@ -179,7 +186,7 @@
     kbuf[own_b, pl.ds(LAT, 128)] = onehot
     lat_in.wait()
 
-    pl.semaphore_wait(bar, 1 + 7 + 30)
+    pl.semaphore_wait(bar, 1 + 7 + 30 + 8)
 
     for r in range(1, CHIPS):
         row = core * 512 + (CHIPS - r) * T_ATT
@@ -458,15 +465,13 @@
         for p in range(8):
             te = lax.rem(e + OFFSETS[8 * b + p] % N_EXP, N_EXP)
             for k in range(N_CORE):
-                tc = lax.rem(core + k, 2)
+                to, tc = entry(OFFSETS[8 * b + p], k)
                 src = bsend.at[b, tc * 8 + p, :, cols]
                 dst = back_ref.at[core * N_EXP + e, :, cols]
                 if b == 0 and p == 0 and k == 0:
                     pltpu.make_async_copy(src, dst, sem_l.at[12]).start()
                 else:
-                    remote(
-                        src, dst, sem_bs.at[b + h], sem_br.at[b + h], 2 * chip + tc, te
-                    ).start()
+                    remote(src, dst, sem_bs.at[b + h], sem_br.at[b + h], to, te).start()
 
     got(0, "GY")
     forward(0, 0)
@@ -476,18 +481,18 @@
     dk_sib.wait_recv()
     s2b[...] = (dkf[own_k, :] + drec[...].astype(F32)).astype(BF).reshape(CHIPS, T_ATT, LAT)
 
-    def piece(i):
+    def piece(z):
         return (
-            pl.ds(pl.multiple_of(lax.div(i, 4) * 16, 16), 16),
-            pl.ds(pl.multiple_of(lax.rem(i, 4) * 128, 128), 128),
+            pl.ds(pl.multiple_of(lax.div(z, 2) * 16, 16), 16),
+            pl.ds(pl.multiple_of(lax.rem(z, 2) * 256, 256), 256),
         )
 
-    rows_e, lanes_e = piece(e)
-    own_piece = pltpu.make_async_copy(s2b.at[:, rows_e, lanes_e], ebuf.at[15], sem_l.at[10])
+    rows_e, lanes_e = piece(lax.div(e, 2))
+    own_piece = pltpu.make_async_copy(s2b.at[:, rows_e, lanes_e], ebuf.at[7], sem_l.at[10])
     own_piece.start()
-    for i in range(1, N_EXP):
-        te = lax.rem(e + i, N_EXP)
-        rows_t, lanes_t = piece(te)
+    for i in range(1, 8):
+        te = lax.rem(e + 2 * i, N_EXP)
+        rows_t, lanes_t = piece(lax.div(te, 2))
         remote(s2b.at[:, rows_t, lanes_t], ebuf.at[i - 1], sem_ds.at[8], sem_dr.at[8], c, te).start()
 
     got(0, "GlY")
@@ -515,9 +520,9 @@
     to_far_again(0, 0)
 
     own_piece.wait()
-    take(ebuf.at[pl.ds(0, 15)], sem_dr.at[8])
+    take(ebuf.at[pl.ds(0, 7)], sem_dr.at[8])
     tot = ebuf[0].astype(F32)
-    for i in range(1, N_EXP):
+    for i in range(1, 8):
         tot = tot + ebuf[i].astype(F32)
     e8[...] = tot.astype(BF)
     for r in range(1, CHIPS):
@@ -540,19 +545,21 @@
     for r in range(CHIPS - 1):
         tot = tot + rbuf[r].astype(F32)
     f1[...] = tot.astype(BF)
-    own_final = pltpu.make_async_copy(f1, dlat.at[rows_e, lanes_e], sem_l.at[11])
+    own_final = pltpu.make_async_copy(f1, gbuf.at[e], sem_l.at[11])
     own_final.start()
     for i in range(1, N_EXP):
         te = lax.rem(e + i, N_EXP)
-        remote(f1, dlat.at[rows_e, lanes_e], sem_ds.at[9], sem_dr.at[9], c, te).start()
+        remote(f1, gbuf.at[e], sem_ds.at[9], sem_dr.at[9], c, te).start()
     dq_ref[...] = dqs[...].reshape(T_ATT, 4, LAT)
 
     give_back(1, 0)
     give_back(1, 1)
 
     own_final.wait()
-    take(ebuf.at[pl.ds(0, 15), 0], sem_dr.at[9])
-    dlat_ref[...] = dlat[...]
+    take(gbuf.at[pl.ds(0, 15)], sem_dr.at[9])
+    for z in range(8):
+        both = gbuf[2 * z].astype(F32) + gbuf[2 * z + 1].astype(F32)
+        dlat_ref[pl.ds(z // 2 * 16, 16), pl.ds(z % 2 * 256, 256)] = both.astype(BF)
 
     for b in range(2):
         for arr in range(2):
@@ -568,9 +575,9 @@
     for cp in sends.values():
         cp.wait_send()
     dk_sib.wait_send()
-    take(ebuf.at[pl.ds(0, 15)], sem_ds.at[8])
+    take(ebuf.at[pl.ds(0, 7)], sem_ds.at[8])
     take(rbuf, sem_ds.at[1])
-    take(ebuf.at[pl.ds(0, 15), 0], sem_ds.at[9])
+    take(gbuf.at[pl.ds(0, 15)], sem_ds.at[9])
     pltpu.make_async_copy(bsend.at[0, 0], back_ref.at[0], sem_l.at[12]).wait()
     for sems in (sem_bs, sem_br):
         take(incoming(bsend, 0), sems.at[0])
@@ -629,11 +636,11 @@
             v(16 * T_ATT, LAT),
             v(CHIPS * T_ATT, LAT),
             v(CHIPS, T_ATT, LAT),
-            v(16, CHIPS, 16, 128),
-            v(CHIPS, 16, 128),
-            v(CHIPS - 1, 16, 128),
-            v(16, 128),
-            v(T_ATT, LAT),
+            v(8, CHIPS, 16, 256),
+            v(CHIPS, 16, 256),
+            v(CHIPS - 1, 16, 256),
+            v(16, 256),
+            v(N_EXP, 16, 256),
             dma((13,)),
             dma((4,)),
             dma((4,)),

time: 139 us -> 122 us (0.88)
  Pallas kernels: 138 us -> 121 us
    pallas_call x1, Pallas kernels: 134 us -> 118 us  [fused(): pl.pallas_call(kernel, out_shape=(jax.ShapeDtypeStruct((PAIRS, 2, OUTW),...]
where the time goes in v4:
time: 122 us
  Pallas kernels  121 us (99%)
    pallas_call x1, Pallas kernels, fused(): pl.pallas_call(kernel, out_shape=(jax.ShapeDtypeStruct((PAIRS, 2, OUTW),...  118 us
    pallas_call x1, Pallas kernels, combine(): pl.pallas_call(combine_kernel, grid=(2,), out_shape=(jax.ShapeDtypeStruct...  3.58 us

profile of v4, /device:TPU:1, one launch (start us, length us, event | category | flops | bytes accessed | tf_op | source)
XLA Modules:
  0.0 121.9 jit_solution(2919213107546786302)
XLA Ops:
  0.6 117.7 %fused.1 = (bf16[32,2,3712]{2,1,0:T(2,128)(2,1)}, bf16[64,4,512]{2,1,0:T(4,128)(2,1)}, bf16[64,512]{1,0:T(8,128)(2,1)}) custom-call(s32[8,128]{1,0:T(8,128)} %bitcast.10, s32[1,128]{1,0:T(1,128)} %prio_ref.3, s32[1,64]{1,0:T(1,128)} %bitcast.13, bf16[128,7168]{1,0:T(8,128)(2,1)} %tok_hbm.1, bf16[128,7168]{1,0:T(8,128)(2,1)} %grd_hbm.1, ...), custom_call_target="tpu_custom_call" | custom-call | tf_op jit(solution)/shard_map/fused/pallas_call | solution.py:596
  118.3 3.6 %combine.1 = (bf16[128,7168]{1,0:T(8,128)(2,1)}, bf16[8,128]{1,0:T(8,128)(2,1)}, bf16[64,4,512]{2,1,0:T(4,128)(2,1)}, bf16[64,512]{1,0:T(8,128)(2,1)}) custom-call(s32[8,128]{1,0:T(8,128)} %bitcast.11, s32[1,128]{1,0:T(1,128)} %prio_ref.3, f32[8,128]{1,0:T(8,128)} %bitcast.12, bf16[32,2,3712]{2,1,0:T(2,128)(2,1)} %get-tuple-element.11.back_ref, ...), custom_call_target="tpu_custom_call" | custom-call | tf_op jit(solution)/shard_map/combine/pallas_call | solution.py:700

commit v5 on v4

--- a/solution.py
+++ b/solution.py
@@ -28,7 +28,8 @@
 STEP = 256
 HB = BLK // 2
 OFFSETS = (0, 1, -1, 2, -2, 3, -3, 4, -4, 5, -5, 6, -6, 7, -7, 8)
-COLS = (((0, OUTW),), ((0, EXTRA + HALF // 2), (EXTRA + HALF // 2, HALF // 2)))
+COLS = (((0, OUTW),), ((0, 1152), (1152, 1024), (2176, 768), (2944, 768)))
+PIECES = len(COLS[0]) + len(COLS[1])
 
 
 def nt(a, b):
@@ -66,7 +67,7 @@
 def kernel(
     ids_ref, prio_ref, docs_ref, tok_hbm, grd_hbm, wg_hbm, wu_hbm, wd_hbm, lat_hbm, q_hbm, do_hbm,
     back_ref, dq_ref, dlat_ref,
-    rows_v, snd, ra, xg, wg, wu, wd, pbuf, prec, ggb, ugb, parts, rsx, rsm, s2p, rsf, rs2, ysend, rsy, bsend,
+    rows_v, snd, ra, xg, wg, wu, wd, pbuf, prec, ggb, ugb, parts, rsx, rsd, rsm, s2p, s3p, rsf, rs2, ysend, rsy, bsend,
     q3, do3, qs, dos, qd, dqs, kbuf, dsb, pwb, dkf, dkb, drec, s2b, ebuf, e8, rbuf, f1, gbuf,
     sem_l, sem_as, sem_ar, sem_ks, sem_kr, sem_ws, sem_wr, sem_gs, sem_gr, sem_ps, sem_pr,
     sem_rs, sem_rr, sem_bs, sem_br, sem_ds, sem_dr,
@@ -344,7 +345,7 @@
     sends = {}
 
     def pass_on(kind, b, h, src, dst, to):
-        index = 3 * kind + b + h
+        index = PIECES * kind + len(COLS[0]) * b + h
         cols = pl.ds(*COLS[b][h])
         sends[kind, b, h] = remote(
             src.at[:, cols], dst.at[:, cols], sem_rs.at[index], sem_rr.at[index], to, e
@@ -415,10 +416,12 @@
     lo, hi = pl.ds(0, HB // 2), pl.ds(HB // 2, HB // 2)
 
     def to_right(b, h):
-        pass_on(0, b, h, parts.at[b, 1], rsx.at[b, 0], right)
+        pass_on(0, b, h, parts.at[b, 1, theirs], rsx.at[b, 0], right)
+        pass_on(8, b, h, parts.at[b, 1, hi], rsd.at[b, hi], right)
 
     def to_left(b, h):
-        pass_on(1, b, h, parts.at[b, 3], rsx.at[b, 1], left)
+        pass_on(1, b, h, parts.at[b, 3, theirs], rsx.at[b, 1], left)
+        pass_on(9, b, h, parts.at[b, 3, lo], rsd.at[b, lo], left)
 
     def to_mate(b, h):
         pass_on(2, b, h, parts.at[b, 2, theirs], rsm.at[b], mate)
@@ -426,9 +429,7 @@
     def to_mate_sum(b, h):
         passed(0, b, h)
         passed(1, b, h)
-        merge_into(
-            b, h, ysend.at[b], [parts.at[b, 0, theirs], rsx.at[b, 0, theirs], rsx.at[b, 1, theirs]]
-        )
+        merge_into(b, h, ysend.at[b], [parts.at[b, 0, theirs], rsx.at[b, 0], rsx.at[b, 1]])
         pass_on(3, b, h, ysend.at[b], rsy.at[b], mate)
 
     def to_far(b, h):
@@ -439,9 +440,11 @@
 
     def to_far_again(b, h):
         passed(4, b, h)
-        pass_on(6, b, h, rsf.at[b, 0], rs2.at[b, lo], right)
+        merge_into(b, h, s3p.at[b, lo], [parts.at[b, 1, lo], rsf.at[b, 0]])
+        pass_on(6, b, h, s3p.at[b, lo], rs2.at[b, lo], right)
         passed(5, b, h)
-        pass_on(7, b, h, rsf.at[b, 1], rs2.at[b, hi], left)
+        merge_into(b, h, s3p.at[b, hi], [parts.at[b, 3, hi], rsf.at[b, 1]])
+        pass_on(7, b, h, s3p.at[b, hi], rs2.at[b, hi], left)
 
     def give_back(b, h):
         def put(cols, val):
@@ -451,6 +454,8 @@
             val = jnp.broadcast_to(score, (HB, EXTRA)).astype(BF)
             bsend[b, :, :, pl.ds(0, EXTRA)] = val.reshape(16, 2, EXTRA)
 
+        passed(8, b, h)
+        passed(9, b, h)
         passed(3, b, h)
         passed(6, b, h)
         passed(7, b, h)
@@ -459,7 +464,7 @@
             h,
             put,
             put_score,
-            [parts.at[b, 0, mine], rsx.at[b, 0, mine], rsx.at[b, 1, mine], rsy.at[b], rs2.at[b]],
+            [parts.at[b, 0, mine], rsd.at[b], rsy.at[b], rs2.at[b]],
         )
         cols = pl.ds(*COLS[b][h])
         for p in range(8):
@@ -469,9 +474,10 @@
                 src = bsend.at[b, tc * 8 + p, :, cols]
                 dst = back_ref.at[core * N_EXP + e, :, cols]
                 if b == 0 and p == 0 and k == 0:
-                    pltpu.make_async_copy(src, dst, sem_l.at[12]).start()
+                    pltpu.make_async_copy(src, dst, sem_l.at[12 + h]).start()
                 else:
-                    remote(src, dst, sem_bs.at[b + h], sem_br.at[b + h], to, te).start()
+                    sem = len(COLS[0]) * b + h
+                    remote(src, dst, sem_bs.at[sem], sem_br.at[sem], to, te).start()
 
     got(0, "GY")
     forward(0, 0)
@@ -509,15 +515,18 @@
     got(1, "GY")
     forward(1, 0)
     hops_third(1)
-    to_mate_sum(0, 0)
-    to_far(0, 0)
+    for h in range(len(COLS[0])):
+        to_mate_sum(0, h)
+    for h in range(len(COLS[0])):
+        to_far(0, h)
     got(1, "GlY")
     forward(1, 3)
     got(1, "GrY")
     forward(1, 1)
     backward(1, 3, to_left)
     backward(1, 1, to_right)
-    to_far_again(0, 0)
+    for h in range(len(COLS[0])):
+        to_far_again(0, h)
 
     own_piece.wait()
     take(ebuf.at[pl.ds(0, 7)], sem_dr.at[8])
@@ -527,18 +536,18 @@
     e8[...] = tot.astype(BF)
     for r in range(1, CHIPS):
         remote(e8.at[r], rbuf.at[CHIPS - 1 - r], sem_ds.at[1], sem_dr.at[1], chip_at(r), e).start()
-    backward(1, 0, None)
-
     got(1, "ThR", "ThL", "T1hR", "T1hL", "Gh0Y", "Gh1Y")
     forward(1, 2)
-    to_mate_sum(1, 0)
     backward(1, 2, to_mate)
-    give_back(0, 0)
-    to_far(1, 0)
-    to_far(1, 1)
-    to_mate_sum(1, 1)
-    to_far_again(1, 0)
-    to_far_again(1, 1)
+    backward(1, 0, None)
+    for h in range(len(COLS[0])):
+        give_back(0, h)
+    for h in range(len(COLS[1])):
+        to_far(1, h)
+    for h in range(len(COLS[1])):
+        to_mate_sum(1, h)
+    for h in range(len(COLS[1])):
+        to_far_again(1, h)
 
     take(rbuf, sem_dr.at[1])
     tot = e8[0].astype(F32)
@@ -552,8 +561,8 @@
         remote(f1, gbuf.at[e], sem_ds.at[9], sem_dr.at[9], c, te).start()
     dq_ref[...] = dqs[...].reshape(T_ATT, 4, LAT)
 
-    give_back(1, 0)
-    give_back(1, 1)
+    for h in range(len(COLS[1])):
+        give_back(1, h)
 
     own_final.wait()
     take(gbuf.at[pl.ds(0, 15)], sem_dr.at[9])
@@ -578,11 +587,14 @@
     take(ebuf.at[pl.ds(0, 7)], sem_ds.at[8])
     take(rbuf, sem_ds.at[1])
     take(gbuf.at[pl.ds(0, 15)], sem_ds.at[9])
-    pltpu.make_async_copy(bsend.at[0, 0], back_ref.at[0], sem_l.at[12]).wait()
-    for sems in (sem_bs, sem_br):
-        take(incoming(bsend, 0), sems.at[0])
-        for h in range(2):
-            take(bsend.at[1, :, :, pl.ds(*COLS[1][h])], sems.at[1 + h])
+    for b in range(2):
+        for h, (start, n) in enumerate(COLS[b]):
+            cols = pl.ds(start, n)
+            if b == 0:
+                own = bsend.at[0, 0, :, cols], back_ref.at[0, :, cols]
+                pltpu.make_async_copy(*own, sem_l.at[12 + h]).wait()
+            for sems in (sem_bs, sem_br):
+                take(bsend.at[b, pl.ds(0, 15 + b), :, cols], sems.at[len(COLS[0]) * b + h])
 
 
 def fused(ids, prio, docs, tok, grd, wg, wu, wd, lat, q, do):
@@ -615,7 +627,9 @@
             v(2 * HB, HID2),
             v(2 * HB, HID2),
             v(2, N_X, 2 * HB, OUTW),
-            v(2, 2, 2 * HB, OUTW),
+            v(2, 2, HB, OUTW),
+            v(2, HB, OUTW),
+            v(2, HB, OUTW),
             v(2, HB, OUTW),
             v(2, HB, OUTW),
             v(2, 2, HB // 2, OUTW),
@@ -641,7 +655,7 @@
             v(CHIPS - 1, 16, 256),
             v(16, 256),
             v(N_EXP, 16, 256),
-            dma((13,)),
+            dma((12 + len(COLS[0]),)),
             dma((4,)),
             dma((4,)),
             dma((2,)),
@@ -652,10 +666,10 @@
             dma((36,)),
             dma((8,)),
             dma((8,)),
-            dma((24,)),
-            dma((24,)),
-            dma((3,)),
-            dma((3,)),
+            dma((10 * PIECES,)),
+            dma((10 * PIECES,)),
+            dma((PIECES,)),
+            dma((PIECES,)),
             dma((10,)),
             dma((10,)),
         ],

time: 122 us -> 120 us (0.984)
  Pallas kernels: 121 us -> 119 us
    pallas_call x1, Pallas kernels: 118 us -> 115 us  [fused(): pl.pallas_call(kernel, out_shape=(jax.ShapeDtypeStruct((PAIRS, 2, OUTW),...]
where the time goes in v5:
time: 120 us; the launch traced here: 119 us
  Pallas kernels  119 us (99%)
    pallas_call x1, Pallas kernels, fused(): pl.pallas_call(kernel, out_shape=(jax.ShapeDtypeStruct((PAIRS, 2, OUTW),...  115 us
    pallas_call x1, Pallas kernels, combine(): pl.pallas_call(combine_kernel, grid=(2,), out_shape=(jax.ShapeDtypeStruct...  3.58 us

profile of v5, /device:TPU:1, one launch (start us, length us, event | category | flops | bytes accessed | tf_op | source)
XLA Modules:
  0.0 119.2 jit_solution(1025337428972505623)
XLA Ops:
  0.6 115.0 %fused.1 = (bf16[32,2,3712]{2,1,0:T(2,128)(2,1)}, bf16[64,4,512]{2,1,0:T(4,128)(2,1)}, bf16[64,512]{1,0:T(8,128)(2,1)}) custom-call(s32[8,128]{1,0:T(8,128)} %bitcast.10, s32[1,128]{1,0:T(1,128)} %prio_ref.3, s32[1,64]{1,0:T(1,128)} %bitcast.13, bf16[128,7168]{1,0:T(8,128)(2,1)} %tok_hbm.1, bf16[128,7168]{1,0:T(8,128)(2,1)} %grd_hbm.1, ...), custom_call_target="tpu_custom_call" | custom-call | tf_op jit(solution)/shard_map/fused/pallas_call | solution.py:608
  115.6 3.6 %combine.1 = (bf16[128,7168]{1,0:T(8,128)(2,1)}, bf16[8,128]{1,0:T(8,128)(2,1)}, bf16[64,4,512]{2,1,0:T(4,128)(2,1)}, bf16[64,512]{1,0:T(8,128)(2,1)}) custom-call(s32[8,128]{1,0:T(8,128)} %bitcast.11, s32[1,128]{1,0:T(1,128)} %prio_ref.3, f32[8,128]{1,0:T(8,128)} %bitcast.12, bf16[32,2,3712]{2,1,0:T(2,128)(2,1)} %get-tuple-element.11.back_ref, ...), custom_call_target="tpu_custom_call" | custom-call | tf_op jit(solution)/shard_map/combine/pallas_call | solution.py:714

commit v6 on v5

--- a/solution.py
+++ b/solution.py
@@ -536,6 +536,7 @@
     e8[...] = tot.astype(BF)
     for r in range(1, CHIPS):
         remote(e8.at[r], rbuf.at[CHIPS - 1 - r], sem_ds.at[1], sem_dr.at[1], chip_at(r), e).start()
+    dq_ref[...] = dqs[...].reshape(T_ATT, 4, LAT)
     got(1, "ThR", "ThL", "T1hR", "T1hL", "Gh0Y", "Gh1Y")
     forward(1, 2)
     backward(1, 2, to_mate)
@@ -546,8 +547,6 @@
         to_far(1, h)
     for h in range(len(COLS[1])):
         to_mate_sum(1, h)
-    for h in range(len(COLS[1])):
-        to_far_again(1, h)
 
     take(rbuf, sem_dr.at[1])
     tot = e8[0].astype(F32)
@@ -559,7 +558,9 @@
     for i in range(1, N_EXP):
         te = lax.rem(e + i, N_EXP)
         remote(f1, gbuf.at[e], sem_ds.at[9], sem_dr.at[9], c, te).start()
-    dq_ref[...] = dqs[...].reshape(T_ATT, 4, LAT)
+    for h in range(len(COLS[1])):
+        to_far_again(1, h)
+
 
     for h in range(len(COLS[1])):
         give_back(1, h)

time: 120 us -> 119 us (level)
  Pallas kernels: 119 us -> 116 us
    pallas_call x1, Pallas kernels: 115 us -> 113 us  [fused(): pl.pallas_call(kernel, out_shape=(jax.ShapeDtypeStruct((PAIRS, 2, OUTW),...]
where the time goes in v6:
time: 119 us; the launch traced here: 117 us
  Pallas kernels  116 us (97%)
    pallas_call x1, Pallas kernels, fused(): pl.pallas_call(kernel, out_shape=(jax.ShapeDtypeStruct((PAIRS, 2, OUTW),...  113 us
    pallas_call x1, Pallas kernels, combine(): pl.pallas_call(combine_kernel, grid=(2,), out_shape=(jax.ShapeDtypeStruct...  3.58 us

profile of v6, /device:TPU:1, one launch (start us, length us, event | category | flops | bytes accessed | tf_op | source)
XLA Modules:
  0.0 117.1 jit_solution(11677616554955987630)
XLA Ops:
  0.6 112.9 %fused.1 = (bf16[32,2,3712]{2,1,0:T(2,128)(2,1)}, bf16[64,4,512]{2,1,0:T(4,128)(2,1)}, bf16[64,512]{1,0:T(8,128)(2,1)}) custom-call(s32[8,128]{1,0:T(8,128)} %bitcast.10, s32[1,128]{1,0:T(1,128)} %prio_ref.3, s32[1,64]{1,0:T(1,128)} %bitcast.13, bf16[128,7168]{1,0:T(8,128)(2,1)} %tok_hbm.1, bf16[128,7168]{1,0:T(8,128)(2,1)} %grd_hbm.1, ...), custom_call_target="tpu_custom_call" | custom-call | tf_op jit(solution)/shard_map/fused/pallas_call | solution.py:609
  113.5 3.6 %combine.1 = (bf16[128,7168]{1,0:T(8,128)(2,1)}, bf16[8,128]{1,0:T(8,128)(2,1)}, bf16[64,4,512]{2,1,0:T(4,128)(2,1)}, bf16[64,512]{1,0:T(8,128)(2,1)}) custom-call(s32[8,128]{1,0:T(8,128)} %bitcast.11, s32[1,128]{1,0:T(1,128)} %prio_ref.3, f32[8,128]{1,0:T(8,128)} %bitcast.12, bf16[32,2,3712]{2,1,0:T(2,128)(2,1)} %get-tuple-element.11.back_ref, ...), custom_call_target="tpu_custom_call" | custom-call | tf_op jit(solution)/shard_map/combine/pallas_call | solution.py:715
